TPU v7x, 512 devices: a whole 4x4x16 slice. The times are simulated.
512 devices in a mesh: outer: 32 (over z, x_hi), inner: 16 (over x_lo, y, core).
Axes of the slice: x: 4 (x_hi: 2, x_lo: 2; x = x_hi * 2 + x_lo), y: 4, z: 16, core: 2. Of those that a mesh axis runs over, the one named last changes fastest.
Arguments:
- fine_input: bfloat16 [98304, 2048], P(('outer', 'inner')), may hold values from -12 to 12
- fine_query: bfloat16 [98304, 1024], P(('outer', 'inner')), may hold values from -4.5 to 4.5
- fine_key: bfloat16 [98304, 1024], P(('outer', 'inner')), may hold values from -4.5 to 4.5
- fine_value: bfloat16 [98304, 1024], P(('outer', 'inner')), may hold values from -6 to 6
- w_fine_out: bfloat16 [1024, 2048], P(None, 'inner'), may hold values from -0.1875 to 0.1875
- norm_gain: float32 [2048], replicated, may hold values from 0.25 to 1.75
- w_query: bfloat16 [2048, 2048], P(None, 'inner'), may hold values from -1 to 1
- w_key: bfloat16 [2048, 2048], P(None, 'inner'), may hold values from -1 to 1
- w_value: bfloat16 [2048, 2048], P(None, 'inner'), may hold values from -0.125 to 0.125
- w_coarse_out: bfloat16 [2048, 2048], P('inner'), may hold values from -0.125 to 0.125
Outputs:
- mixed_stream: bfloat16 [98304, 2048], P(('outer', 'inner'))
All inputs are finite; a program needn't handle non-finite values.
Results may differ from a plain program's by a relative error of at most 0.008.
Values may be sent and summed in bfloat16 or wider, within the bound.
A program may use at most 128 MiB of HBM per device.

v0:
```python
import math

import jax
import jax.numpy as jnp
from jax import lax
from jax.sharding import PartitionSpec as P

HE = 128
WIN = 512
POOL = 8


very_negative = -1e30


def passed_along(block, axis, distance):
    devices = range(lax.axis_size(axis))
    route = [(i - distance, i) for i in devices if i - distance in devices]
    return lax.ppermute(block, axis, route)


def joined_along(blocks, dim):
    lengths = list(blocks.shape[1:])
    lengths[dim] *= blocks.shape[0]
    return jnp.moveaxis(blocks, 0, dim).reshape(lengths)


def copy_for_each(shard, axis):
    copies = jnp.broadcast_to(shard, (lax.axis_size(axis), *shard.shape))
    return lax.all_to_all(copies, axis, split_axis=0, concat_axis=0, tiled=True)


def gather_directly(shard, axis, dim):
    return joined_along(copy_for_each(shard, axis), dim)


def sent_together(arrays, axis, dim, along):
    both = jnp.concatenate(arrays, axis=along)
    out, at, outs = (lax.all_gather(both, axis, axis=dim, tiled=True), 0, [])
    for a in arrays:
        outs.append(lax.slice_in_dim(out, at, at + a.shape[along], axis=along))
        at += a.shape[along]
    return tuple(outs)


def cut_along(shard, dim, size):
    lengths = shard.shape
    blocks = shard.reshape(*lengths[:dim], size, lengths[dim] // size, *lengths[dim + 1 :])
    return jnp.moveaxis(blocks, dim, 0)


def summed_on_arrival(shard, axis, dim):
    blocks = cut_along(shard, dim, lax.axis_size(axis))
    arrived = lax.all_to_all(blocks, axis, split_axis=0, concat_axis=0, tiled=True)
    return arrived.astype(jnp.float32).sum(axis=0)


def on_device(
    fine_input,
    fine_query,
    fine_key,
    fine_value,
    w_fine_out,
    norm_gain,
    w_query,
    w_key,
    w_value,
    w_coarse_out,
):
    tok_rows, model_width = fine_input.shape
    fine_heads = fine_query.shape[1] // HE
    score_scale = 1.0 / math.sqrt(HE)
    reach_count = (WIN + tok_rows - 1) // tok_rows
    position = lax.axis_index(("outer", "inner"))
    key_list = []
    value_list = []
    for distance in range(reach_count, 0, -1):
        shifted = passed_along((fine_key, fine_value), ("outer", "inner"), distance)
        key_list.append(shifted[0])
        value_list.append(shifted[1])
    key_list.append(fine_key)
    value_list.append(fine_value)
    span = (reach_count + 1) * tok_rows
    key_heads = jnp.concatenate(key_list, axis=0).reshape(span, fine_heads, HE)
    value_heads = jnp.concatenate(value_list, axis=0).reshape(span, fine_heads, HE)
    query_heads = fine_query.reshape(tok_rows, fine_heads, HE)
    scores = (
        jnp.einsum("qhe,khe->hqk", query_heads, key_heads, preferred_element_type=jnp.float32)
        * score_scale
    )
    row_ids = jnp.arange(tok_rows, dtype=jnp.int32)[:, None] + reach_count * tok_rows
    col_ids = jnp.arange(span, dtype=jnp.int32)[None, :]
    gap_rows = row_ids - col_ids
    allowed = (
        (gap_rows >= 0) & (gap_rows < WIN) & ((position - reach_count) * tok_rows + col_ids >= 0)
    )
    masked = jnp.where(allowed[None], scores, very_negative)
    row_max = jnp.max(masked, axis=-1, keepdims=True)
    exp_weights = jnp.where(allowed[None], jnp.exp(scores - row_max), 0.0)
    row_sum = jnp.sum(exp_weights, axis=-1)
    summed = jnp.einsum(
        "hqk,khe->qhe",
        exp_weights.astype(jnp.bfloat16),
        value_heads,
        preferred_element_type=jnp.float32,
    )
    fine_mix = (
        (summed / jnp.transpose(row_sum)[:, :, None])
        .astype(jnp.bfloat16)
        .reshape(tok_rows, fine_heads * HE)
    )
    projected = jnp.dot(
        fine_mix,
        lax.all_gather(w_fine_out, "inner", axis=1, tiled=True),
        preferred_element_type=jnp.float32,
    )
    fine_state = (fine_input.astype(jnp.float32) + projected).astype(jnp.bfloat16)
    edge_rows = passed_along(fine_state[tok_rows - POOL + 1 :], ("outer", "inner"), 1)
    first_pool = (
        jnp.sum(edge_rows, axis=0, dtype=jnp.float32) + fine_state[0].astype(jnp.float32)
    ) / POOL
    later_pools = (
        jnp.sum(
            fine_state[1 : tok_rows - POOL + 1].reshape(tok_rows // POOL - 1, POOL, model_width),
            axis=1,
            dtype=jnp.float32,
        )
        / POOL
    )
    pooled = jnp.concatenate([first_pool[None], later_pools], axis=0).astype(jnp.bfloat16)
    pooled_wide = pooled.astype(jnp.float32)
    moment = jnp.mean(pooled_wide * pooled_wide, axis=-1, keepdims=True)
    normed = (pooled_wide * lax.rsqrt(moment + 1e-06) * norm_gain).astype(jnp.bfloat16)
    local_heads = w_query.shape[1] // HE
    head_width = local_heads * HE
    joined_weights = jnp.concatenate([w_query, w_key, w_value], axis=1)
    projections = jnp.dot(
        gather_directly(normed, "inner", 0), joined_weights, preferred_element_type=jnp.float32
    ).astype(jnp.bfloat16)
    group_len = projections.shape[0]
    coarse_query = projections[:, :head_width].reshape(group_len, local_heads, HE)
    coarse_key = projections[:, head_width : 2 * head_width]
    coarse_value = projections[:, 2 * head_width :]
    outer_index = lax.axis_index("outer")
    query_pos = outer_index * group_len + jnp.arange(group_len, dtype=jnp.int32)
    last_query = outer_index * group_len + group_len - 1

    def attend(running, pieces):
        prior_max, prior_sum, prior_acc = running
        count = pieces[0].shape[0]
        block_keys = pieces[0].reshape(count, local_heads, HE)
        block_values = pieces[1].reshape(count, local_heads, HE)
        block_scores = (
            jnp.einsum("qhe,khe->hqk", coarse_query, block_keys, preferred_element_type=jnp.float32)
            * score_scale
        )
        key_pos = jnp.arange(count, dtype=jnp.int32)
        visible = (key_pos[None, :] <= query_pos[:, None])[None]
        block_masked = jnp.where(visible, block_scores, very_negative)
        new_max = jnp.maximum(prior_max, jnp.max(block_masked, axis=-1))
        block_exp = jnp.where(visible, jnp.exp(block_scores - new_max[:, :, None]), 0.0)
        new_sum = jnp.sum(block_exp, axis=-1)
        contrib = jnp.einsum(
            "hqk,khe->hqe",
            block_exp.astype(jnp.bfloat16),
            block_values,
            preferred_element_type=jnp.float32,
        )
        return (new_max, new_sum, contrib)

    start_state = (
        jnp.full((local_heads, group_len), very_negative, jnp.float32),
        jnp.zeros((local_heads, group_len), jnp.float32),
        jnp.zeros((local_heads, group_len, HE), jnp.float32),
    )
    pieces = sent_together((coarse_key, coarse_value), "outer", 0, 1)
    final_max, final_sum, final_acc = lax.cond(
        jnp.int32(0) <= last_query, lambda: attend(start_state, pieces), lambda: start_state
    )
    coarse_mix = (
        jnp.transpose(final_acc / final_sum[:, :, None], (1, 0, 2))
        .reshape(group_len, head_width)
        .astype(jnp.bfloat16)
    )
    head_total = summed_on_arrival(
        jnp.dot(coarse_mix, w_coarse_out, preferred_element_type=jnp.float32).astype(jnp.bfloat16),
        "inner",
        0,
    )
    coarse_out = (pooled_wide + head_total).astype(jnp.bfloat16)
    fine_groups = fine_state.reshape(tok_rows // POOL, POOL, model_width).astype(jnp.float32)
    lifted = fine_groups + coarse_out.astype(jnp.float32)[:, None, :]
    return lifted.reshape(tok_rows, model_width).astype(jnp.bfloat16)


def solution(mesh):
    placed = (
        P(("outer", "inner"), None),
        P(("outer", "inner"), None),
        P(("outer", "inner"), None),
        P(("outer", "inner"), None),
        P(None, "inner"),
        P(),
        P(None, "inner"),
        P(None, "inner"),
        P(None, "inner"),
        P("inner", None),
    )
    return jax.shard_map(
        on_device,
        mesh=mesh,
        in_specs=placed,
        out_specs=P(("outer", "inner"), None),
        check_vma=False,
    )
```

profile of v0, /device:TPU:1, one launch (start us, length us, event | category | flops | bytes accessed | tf_op | source)
XLA Modules:
  0.0 392.4 jit_solution(16497863466739986728)
XLA Ops:
  6.5 0.7 all-gather.3.cloned.1.call-update
  7.3 1.2 copy.12
  8.5 4.6 %collective-permute-start.2 = (bf16[192,1024]{0,1:T(8,128)(2,1)S(1)}, bf16[192,1024]{0,1:T(8,128)(2,1)S(1)}, u32[]{:S(2)}, u32[]{:S(2)}) collective-permute-start(bf16[192,1024]{0,1:T(8,128)(2,1)S(1)} %copy.12), channel_id=1, source_target_pairs={{0,1},{1,2},{2,3},{3,4},{4,5},{5,6},{6,7},{7,8},{8,9},{9,10},{10,1... | collective-permute-start | bytes 1179656 | tf_op jit(solution)/shard_map/ppermute | solution.py:19
  13.1 3.2 collective-permute-start.1
  16.3 4.3 %collective-permute-start = (bf16[192,1024]{0,1:T(8,128)(2,1)S(1)}, bf16[192,1024]{0,1:T(8,128)(2,1)}, u32[]{:S(2)}, u32[]{:S(2)}) collective-permute-start(bf16[192,1024]{0,1:T(8,128)(2,1)S(1)} %copy.12), channel_id=1, source_target_pairs={{0,3},{1,4},{2,5},{3,6},{4,7},{5,8},{6,9},{7,10},{8,11},{9,12},{10... | collective-permute-start | bytes 1179656 | tf_op jit(solution)/shard_map/ppermute | solution.py:19
  20.6 1.2 copy.16
  21.8 2.4 collective-permute-start.5
  24.3 3.2 collective-permute-start.4
  27.5 3.2 collective-permute-start.3
  31.0 0.8 copy-done.2
  31.8 19.1 %collective-permute-done = bf16[192,1024]{0,1:T(8,128)(2,1)} collective-permute-done((bf16[192,1024]{0,1:T(8,128)(2,1)S(1)}, bf16[192,1024]{0,1:T(8,128)(2,1)}, u32[]{:S(2)}, u32[]{:S(2)}) %collective-permute-start) | collective-permute-done | bytes 393248 | tf_op jit(solution)/shard_map/ppermute | solution.py:19
  50.9 2.1 pad_maximum_fusion
  53.0 16.7 %collective-permute-done.5 = bf16[192,1024]{0,1:T(8,128)(2,1)} collective-permute-done((bf16[192,1024]{0,1:T(8,128)(2,1)S(1)}, bf16[192,1024]{0,1:T(8,128)(2,1)}, u32[]{:S(2)}, u32[]{:S(2)}) %collective-permute-start.5) | collective-permute-done | bytes 393248 | tf_op jit(solution)/shard_map/ppermute | solution.py:19
  69.7 14.1 %collective-permute-done.4 = bf16[192,1024]{0,1:T(8,128)(2,1)} collective-permute-done((bf16[192,1024]{0,1:T(8,128)(2,1)S(1)}, bf16[192,1024]{0,1:T(8,128)(2,1)}, u32[]{:S(2)}, u32[]{:S(2)}) %collective-permute-start.4) | collective-permute-done | bytes 393248 | tf_op jit(solution)/shard_map/ppermute | solution.py:19
  83.8 5.7 %collective-permute-done.3 = bf16[192,1024]{0,1:T(8,128)(2,1)S(1)} collective-permute-done((bf16[192,1024]{0,1:T(8,128)(2,1)S(1)}, bf16[192,1024]{0,1:T(8,128)(2,1)S(1)}, u32[]{:S(2)}, u32[]{:S(2)}) %collective-permute-start.3) | collective-permute-done | bytes 393248 | tf_op jit(solution)/shard_map/ppermute | solution.py:19
  89.5 3.1 pad_maximum_fusion.1
  92.6 5.8 %fusion.77 = (f32[8,192]{1,0:T(8,128)S(1)}, bf16[8,192,768]{2,1,0:T(8,128)(2,1)}) fusion(pred[192,768]{1,0:T(8,128)(4,1)S(1)} %fusion.49, bf16[768,8,128]{0,2,1:T(8,128)(2,1)} %bitcast.77, bf16[192,1024]{1,0:T(8,128)(2,1)} %param.13), kind=kOutput, calls=%fused_computation.83 | convolution fusion | flops 612238080 | bytes 4478976 | tf_op jit(solution)/shard_map/sub | solution.py:99
  98.4 2.4 fusion.43
  100.9 3.4 fusion.18
  104.9 1.9 collective-permute-start.6
  106.8 1.2 collective-permute-done.6
  108.5 36.4 %all_to_all.10 = bf16[16,24,2048]{2,1,0:T(8,128)(2,1)S(1)} all-to-all(bf16[16,24,2048]{2,1,0:T(8,128)(2,1)S(1)} %broadcast_in_dim.55), channel_id=1, replica_groups=mesh['outer'=32,'inner'=16] {'inner'}, dimensions={0} | all-to-all | bytes 3145728 | tf_op jit(solution)/shard_map/all_to_all | solution.py:30
  144.9 1.0 fusion.40
  145.9 0.7 concatenate.25
  146.6 173.0 %all-gather.5.cloned.1.call-done = bf16[12288,256]{1,0:T(8,128)(2,1)} async-done(((bf16[384,256]{1,0:T(8,128)(2,1)}), bf16[12288,256]{1,0:T(8,128)(2,1)}) %all-gather.5.cloned.1.call-update) | async-done | bytes 6291472 | tf_op jit(solution)/shard_map/all_gather | solution.py:39
  319.7 30.4 %conditional.1 = (f32[1,384]{1,0:T(1,128)S(1)}, f32[1,384,128]{2,1,0:T(8,128)S(1)}) conditional(s32[]{:T(128)} %convert_element_type.93, () %tuple.13, (s32[]{:T(128)}, s32[384]{0:T(512)S(1)}, bf16[384,384]{1,0:T(8,128)(2,1)S(1)}, bf16[12288,256]{1,0:T(8,128)(2,1)}) %tuple.14), branch_computations={%region_5.6_spmd, %region_6.9_spmd} | conditional | flops 2472542208 | bytes 63229972 | solution.py:177
  319.7 9.9 %select_reduce_fusion = (f32[384]{0:T(512)S(1)}, f32[384,12288]{1,0:T(8,128)}) fusion(s32[384]{0:T(512)S(1)} %broadcast_add_fusion, bf16[12288,256]{1,0:T(8,128)(2,1)} %get-tuple-element.23, bf16[384,384]{1,0:T(8,128)(2,1)S(1)} %get-tuple-element.22), kind=kOutput, calls=%fused_computation.1 | convolution fusion | flops 1226833536 | bytes 22121984 | tf_op jit(solution)/shard_map/cond/branch_1_fun/qhe,khe->hqk/dot_general | solution.py:154
  329.5 11.1 %fusion.1 = f32[384]{0:T(512)S(1)} fusion(f32[384,12288]{1,0:T(8,128)} %get-tuple-element.29, f32[384]{0:T(512)S(1)} %broadcast_maximum_fusion, s32[384]{0:T(512)S(1)} %broadcast_add_fusion), kind=kLoop, calls=%fused_computation.5 | loop fusion | flops 18873984 | bytes 18878976 | tf_op jit(solution)/shard_map/cond/branch_1_fun/reduce_sum | solution.py:162
  340.6 9.5 %fusion.6 = f32[1,384,128]{2,1,0:T(8,128)S(1)} fusion(bf16[12288,256]{1,0:T(8,128)(2,1)} %get-tuple-element.23, f32[384,12288]{1,0:T(8,128)} %get-tuple-element.29, f32[384]{0:T(512)S(1)} %broadcast_maximum_fusion, s32[384]{0:T(512)S(1)} %broadcast_add_fusion), kind=kOutput, calls=%fused_computation.9 | convolution fusion | flops 1226833920 | bytes 22219776 | tf_op jit(solution)/shard_map/cond/branch_1_fun/hqk,khe->hqe/dot_general | solution.py:163
  350.1 0.6 convolution_convert_fusion
  350.7 33.5 %all_to_all.11 = bf16[16,24,2048]{2,1,0:T(8,128)(2,1)S(1)} all-to-all(bf16[16,24,2048]{2,1,0:T(8,128)(2,1)S(1)} %bitcast.75), channel_id=1, replica_groups=mesh['outer'=32,'inner'=16] {'inner'}, dimensions={0} | all-to-all | bytes 3145728 | tf_op jit(solution)/shard_map/all_to_all | solution.py:54
  384.5 1.1 fusion.30
  (38 shorter events, 1.8 us)
Async XLA Ops:
  6.5 343.6 %copy-start = (bf16[128,2048]{1,0:T(8,128)(2,1)S(1)}, bf16[128,2048]{1,0:T(8,128)(2,1)}, u32[]{:S(2)}) copy-start(bf16[128,2048]{1,0:T(8,128)(2,1)} %param.21) | copy-start | bytes 1572868
  6.5 94.3 %all-gather.3.cloned.1.call-start = ((), (), s32[]{:S(2)}) async-start(), calls=%async_computation.2 | async-start | bytes 4456448 | tf_op jit(solution)/shard_map/all_gather | solution.py:114
  7.3 312.4 %all-gather.5.cloned.1.call-start = ((), (), s32[]{:S(2)}) async-start(), calls=%async_computation.3 | async-start | bytes 6488064 | tf_op jit(solution)/shard_map/all_gather | solution.py:39
  8.5 19.0 %collective-permute-start.2 = (bf16[192,1024]{0,1:T(8,128)(2,1)S(1)}, bf16[192,1024]{0,1:T(8,128)(2,1)S(1)}, u32[]{:S(2)}, u32[]{:S(2)}) collective-permute-start(bf16[192,1024]{0,1:T(8,128)(2,1)S(1)} %copy.12), channel_id=1, source_target_pairs={{0,1},{1,2},{2,3},{3,4},{4,5},{5,6},{6,7},{7,8},{8,9},{9,10},{10,1... | collective-permute-start | bytes 1179656 | tf_op jit(solution)/shard_map/ppermute | solution.py:19
  13.1 17.9 %collective-permute-start.1 = (bf16[192,1024]{0,1:T(8,128)(2,1)S(1)}, bf16[192,1024]{0,1:T(8,128)(2,1)S(1)}, u32[]{:S(2)}, u32[]{:S(2)}) collective-permute-start(bf16[192,1024]{0,1:T(8,128)(2,1)S(1)} %copy.12), channel_id=1, source_target_pairs={{0,2},{1,3},{2,4},{3,5},{4,6},{5,7},{6,8},{7,9},{8,10},{9,11},{10,... | collective-permute-start | bytes 1179656 | tf_op jit(solution)/shard_map/ppermute | solution.py:19
  16.3 34.6 %collective-permute-start = (bf16[192,1024]{0,1:T(8,128)(2,1)S(1)}, bf16[192,1024]{0,1:T(8,128)(2,1)}, u32[]{:S(2)}, u32[]{:S(2)}) collective-permute-start(bf16[192,1024]{0,1:T(8,128)(2,1)S(1)} %copy.12), channel_id=1, source_target_pairs={{0,3},{1,4},{2,5},{3,6},{4,7},{5,8},{6,9},{7,10},{8,11},{9,12},{10... | collective-permute-start | bytes 1179656 | tf_op jit(solution)/shard_map/ppermute | solution.py:19
  21.8 47.8 %collective-permute-start.5 = (bf16[192,1024]{0,1:T(8,128)(2,1)S(1)}, bf16[192,1024]{0,1:T(8,128)(2,1)}, u32[]{:S(2)}, u32[]{:S(2)}) collective-permute-start(bf16[192,1024]{0,1:T(8,128)(2,1)S(1)} %copy.16), channel_id=1, source_target_pairs={{0,1},{1,2},{2,3},{3,4},{4,5},{5,6},{6,7},{7,8},{8,9},{9,10},{10,1... | collective-permute-start | bytes 1179656 | tf_op jit(solution)/shard_map/ppermute | solution.py:19
  24.3 59.5 %collective-permute-start.4 = (bf16[192,1024]{0,1:T(8,128)(2,1)S(1)}, bf16[192,1024]{0,1:T(8,128)(2,1)}, u32[]{:S(2)}, u32[]{:S(2)}) collective-permute-start(bf16[192,1024]{0,1:T(8,128)(2,1)S(1)} %copy.16), channel_id=1, source_target_pairs={{0,2},{1,3},{2,4},{3,5},{4,6},{5,7},{6,8},{7,9},{8,10},{9,11},{10,... | collective-permute-start | bytes 1179656 | tf_op jit(solution)/shard_map/ppermute | solution.py:19
  27.5 3.5 copy-start.1
  27.5 61.9 %collective-permute-start.3 = (bf16[192,1024]{0,1:T(8,128)(2,1)S(1)}, bf16[192,1024]{0,1:T(8,128)(2,1)S(1)}, u32[]{:S(2)}, u32[]{:S(2)}) collective-permute-start(bf16[192,1024]{0,1:T(8,128)(2,1)S(1)} %copy.16), channel_id=1, source_target_pairs={{0,3},{1,4},{2,5},{3,6},{4,7},{5,8},{6,9},{7,10},{8,11},{9,12},{10... | collective-permute-start | bytes 1179656 | tf_op jit(solution)/shard_map/ppermute | solution.py:19
  31.0 0.8 copy-start.2
  100.8 7.4 %copy-start.3 = (f32[2048]{0:T(1024)S(1)}, f32[2048]{0:T(1024)}, u32[]{:S(2)}) copy-start(f32[2048]{0:T(1024)} %param.17) | copy-start | bytes 24580
  104.3 40.6 %copy-start.4 = (bf16[2048,128]{1,0:T(8,128)(2,1)S(1)}, bf16[2048,128]{1,0:T(8,128)(2,1)}, u32[]{:S(2)}) copy-start(bf16[2048,128]{1,0:T(8,128)(2,1)} %param.20) | copy-start | bytes 1572868
  104.3 40.6 %copy-start.5 = (bf16[2048,128]{1,0:T(8,128)(2,1)S(1)}, bf16[2048,128]{1,0:T(8,128)(2,1)}, u32[]{:S(2)}) copy-start(bf16[2048,128]{1,0:T(8,128)(2,1)} %param.19) | copy-start | bytes 1572868
  104.3 40.6 %copy-start.6 = (bf16[2048,128]{1,0:T(8,128)(2,1)S(1)}, bf16[2048,128]{1,0:T(8,128)(2,1)}, u32[]{:S(2)}) copy-start(bf16[2048,128]{1,0:T(8,128)(2,1)} %param.18) | copy-start | bytes 1572868
  104.9 3.1 collective-permute-start.6
Sparse Core Ops, SparseCore 0:
  9.4 69.3 all-gather.2
  146.7 172.8 all-gather.4
where the time goes:
time: 393 us; the launch traced here: 392 us
  waiting for transfers between devices  231 us (59%)
  blocking collectives  69.9 us (18%)
  matrix products  32.6 us (8%)
  starting transfers between devices  22.9 us (6%)
  other arithmetic  18.8 us (5%)
  between operations  13.6 us (3%)
  local copies, waits for them, and re-layouts  4.12 us (1%)
    all_gather x1, waiting for transfers between devices, sent_together(): out, at, outs = (lax.all_gather(both, axis, axis=dim, tiled=True), 0, [])  173 us
    ppermute x7, waiting for transfers between devices, passed_along(): return lax.ppermute(block, axis, route)  56.7 us
    all_to_all x1, blocking collectives, copy_for_each(): return lax.all_to_all(copies, axis, split_axis=0, concat_axis=0, tiled=True)  36.4 us
    all_to_all x1, blocking collectives, summed_on_arrival(): lax.all_to_all(blocks, axis, split_axis=0, concat_axis=0, tiled=True)  33.5 us
    ppermute x7, starting transfers between devices, passed_along(): return lax.ppermute(block, axis, route)  22.9 us
    reduce_sum x1, other arithmetic, attend(): new_sum = jnp.sum(block_exp, axis=-1)  11.1 us
    dot_general x1, matrix products, attend(): jnp.einsum('qhe,khe->hqk', coarse_query, block_keys, preferred_element_ty...  9.86 us
    dot_general x1, matrix products, attend(): jnp.einsum('hqk,khe->hqe', block_exp.astype(jnp.bfloat16), block_values,...  9.49 us
  transfers between devices with their start and end apart: 9, of which 6 were waited for; matrix products, arithmetic and copies ran while one was open for 4% of the time, Pallas kernels for 0%

commit v1 on v0

v1 whole, which is shorter than its diff:
```python
import functools
import math

import jax
import jax.numpy as jnp
from jax import lax
from jax.experimental import pallas as pl
from jax.experimental.pallas import tpu as pltpu
from jax.sharding import PartitionSpec as P

HE = 128
WIN = 512
POOL = 8
NEG = -1e30
LOG2E = math.log2(math.e)
SCALE = 1.0 / math.sqrt(HE)
BF = jnp.bfloat16
F32 = jnp.float32
TRANS = (((1,), (1,)), ((), ()))
MESH = pl.DeviceIdType.MESH
NX, NY, NZ, NC = 4, 4, 16, 2
NP = NX * NY * NC


def vmem_spec():
    return pl.BlockSpec(memory_space=pltpu.VMEM)


def any_spec():
    return pl.BlockSpec(memory_space=pl.ANY)


def place():
    outer = lax.axis_index("outer")
    inner = lax.axis_index("inner")
    x = (outer % 2) * 2 + inner // 8
    return x, (inner // 2) % NY, outer // 2, inner % NC


def device_at(x, y, z, c):
    return (z * 2 + x // 2, (x % 2) * 8 + y * 2 + c)


def device_of(pos):
    pos = (pos + 512) % 512
    return (pos // 16, pos % 16)


def slot_of(x, y, c):
    return x * 8 + y * 2 + c


def greet(devices):
    barrier = pltpu.get_barrier_semaphore()
    for d in devices:
        pl.semaphore_signal(barrier, inc=1, device_id=d, device_id_type=MESH)
    pl.semaphore_wait(barrier, len(devices))


def plane_neighbours():
    x, y, z, c = place()
    return [
        device_at((x + 1) % NX, y, z, c),
        device_at((x + 3) % NX, y, z, c),
        device_at(x, (y + 1) % NY, z, c),
        device_at(x, (y + 3) % NY, z, c),
        device_at(x, y, z, 1 - c),
    ]


class Sends:
    def __init__(self, send_sem, recv_sem, base=0):
        self.send_sem, self.recv_sem, self.next = send_sem, recv_sem, base
        self.started = []

    def new(self):
        self.next += 1
        return self.next - 1

    def copy(self, k, src, dst, to):
        return pltpu.make_async_remote_copy(
            src_ref=src,
            dst_ref=dst,
            send_sem=self.send_sem.at[k],
            recv_sem=self.recv_sem.at[k],
            device_id=to,
            device_id_type=MESH,
        )

    def start(self, k, src, dst, to):
        c = self.copy(k, src, dst, to)
        c.start()
        self.started.append(c)

    def arrived(self, k, dst, to):
        self.copy(k, dst, dst, to).wait_recv()

    def drain(self):
        for c in self.started:
            c.wait_send()
        self.started = []


PLANE_COPIES = 71


def plane_gather(sends, src, dst, local_sem):
    x, y, z, c = place()
    rows = src.shape[0]
    quarter = rows // 4

    def xy(axis, off):
        return ((x + off) % NX, y) if axis == 0 else (x, (y + off) % NY)

    def near(axis, off):
        px, py = xy(axis, off)
        return device_at(px, py, z, c)

    def at(axis, a, b):
        if axis == 0:
            return slot_of((x + a) % NX, (y + b) % NY, c)
        return slot_of((x + b) % NX, (y + a) % NY, c)

    partner = device_at(x, y, z, 1 - c)
    halves = []
    for first in (0, 1):
        lo = first * 2 * quarter
        halves.append(
            dict(
                first=first,
                whole=pl.ds(lo, 2 * quarter),
                q0=pl.ds(lo, quarter),
                q1=pl.ds(lo + quarter, quarter),
                k={},
            )
        )
    for h in halves:
        for name in ("r1", "l1", "r2", "l2"):
            h["k"][name] = sends.new()
        for j in (0, -1, 1, 2):
            for name in ("r1", "l1", "r2", "l2"):
                h["k"][name, j] = sends.new()
        for j in (0, -1, 1, 2):
            for i in (0, -1, 1, 2):
                if (i, j) != (0, 0):
                    h["k"]["p", j, i] = sends.new()
    own_pair = sends.new()
    mine = slot_of(x, y, c)
    theirs = slot_of(x, y, 1 - c)
    local = pltpu.make_async_copy(src, dst.at[mine], local_sem)

    def to_partner(h, j, i):
        s = at(h["first"], j, i)
        sends.start(h["k"]["p", j, i], dst.at[s, h["whole"]], dst.at[s, h["whole"]], partner)

    for h in halves:
        a = h["first"]
        for name, off in (("r1", 1), ("l1", -1)):
            sends.start(
                h["k"][name], src.at[h["whole"]], dst.at[mine, h["whole"]], near(a, off % 4)
            )
    for h in halves:
        b = 1 - h["first"]
        for name, off in (("r1", 1), ("l1", -1)):
            sends.start(
                h["k"][name, 0], src.at[h["whole"]], dst.at[mine, h["whole"]], near(b, off % 4)
            )
    sends.start(own_pair, src, dst.at[mine], partner)
    local.start()
    yield

    def second(h, j):
        s = at(h["first"], j, 0)
        for name, off in (("r1", 1), ("l1", -1)):
            sends.start(
                h["k"][name, j],
                dst.at[s, h["whole"]],
                dst.at[s, h["whole"]],
                near(1 - h["first"], off % 4),
            )
        to_partner(h, j, 0)

    for h in halves:
        a = h["first"]
        for name, fwd, off, part in (("r1", "r2", -1, "q0"), ("l1", "l2", 1, "q1")):
            s = at(a, off, 0)
            sends.arrived(h["k"][name], dst.at[s, h["whole"]], near(a, off % 4))
            sends.start(
                h["k"][fwd], dst.at[s, h[part]], dst.at[s, h[part]], near(a, (-off) % 4)
            )
    for h in halves:
        for off in (-1, 1):
            second(h, off)
    yield

    def relay(h, j):
        b = 1 - h["first"]
        for name, fwd, off, part in (("r1", "r2", -1, "q0"), ("l1", "l2", 1, "q1")):
            s = at(h["first"], j, off)
            sends.arrived(h["k"][name, j], dst.at[s, h["whole"]], near(b, off % 4))
            sends.start(
                h["k"][fwd, j], dst.at[s, h[part]], dst.at[s, h[part]], near(b, (-off) % 4)
            )
            to_partner(h, j, off)

    for h in halves:
        relay(h, 0)
    yield
    for h in halves:
        a = h["first"]
        s = at(a, 2, 0)
        sends.arrived(h["k"]["r2"], dst.at[s, h["q0"]], near(a, 3))
        sends.arrived(h["k"]["l2"], dst.at[s, h["q1"]], near(a, 1))
        second(h, 2)
    yield

    def last(h, j):
        b = 1 - h["first"]
        s = at(h["first"], j, 2)
        sends.arrived(h["k"]["r2", j], dst.at[s, h["q0"]], near(b, 3))
        sends.arrived(h["k"]["l2", j], dst.at[s, h["q1"]], near(b, 1))
        to_partner(h, j, 2)

    for j in (-1, 1):
        for h in halves:
            relay(h, j)
    for h in halves:
        last(h, 0)
    yield
    for h in halves:
        relay(h, 2)
    for j in (-1, 1):
        for h in halves:
            last(h, j)
    yield
    for h in halves:
        last(h, 2)
    local.wait()
    sends.arrived(own_pair, dst.at[theirs], partner)
    for h in halves:
        for j in (0, -1, 1, 2):
            for i in (0, -1, 1, 2):
                if (i, j) != (0, 0):
                    s = at(h["first"], j, i) + 1 - 2 * c
                    sends.arrived(h["k"]["p", j, i], dst.at[s, h["whole"]], partner)
    yield


def run_all(steps):
    for _ in steps:
        pass


def gather_kernel(src_ref, dst_ref, local_sem, send_sem, recv_sem):
    greet(plane_neighbours())
    sends = Sends(send_sem, recv_sem)
    run_all(plane_gather(sends, src_ref, dst_ref, local_sem))
    sends.drain()


def gathered_in_plane(block, collective_id):
    return pl.pallas_call(
        gather_kernel,
        out_shape=jax.ShapeDtypeStruct((NP, *block.shape), block.dtype),
        in_specs=[any_spec()],
        out_specs=any_spec(),
        scratch_shapes=[
            pltpu.SemaphoreType.DMA,
            pltpu.SemaphoreType.DMA((PLANE_COPIES,)),
            pltpu.SemaphoreType.DMA((PLANE_COPIES,)),
        ],
        compiler_params=pltpu.CompilerParams(
            collective_id=collective_id, has_side_effects=True, vmem_limit_bytes=16 << 20
        ),
        name=f"plane_gather_{collective_id}",
    )(block)


def halo_kernel(k_ref, v_ref, kp_ref, vp_ref, send_sem, recv_sem):
    x, y, z, c = place()
    pos = lax.axis_index("outer") * 16 + lax.axis_index("inner")
    rows = k_ref.shape[0]
    short = WIN - 2 * rows
    ahead, behind = device_of(pos + 2), device_of(pos - 2)
    partner = device_at(x, y, z, 1 - c)
    greet([ahead, behind, partner, device_of(pos + 3), device_of(pos - 3)])
    sends = Sends(send_sem, recv_sem)
    pairs = ((k_ref, kp_ref), (v_ref, vp_ref))
    mid, end = pl.ds(short, rows), pl.ds(short + rows, rows)
    head, tail = pl.ds(0, short), pl.ds(rows - short, short)
    for n, (own, prev) in enumerate(pairs):
        sends.start(n, own, prev.at[mid], ahead)

    def put(n, src, dst, to):
        sends.copy(n, src, dst, to).start()

    for n, (own, prev) in enumerate(pairs):

        @pl.when(c == 0)
        def _():
            put(2 + n, own, prev.at[end], partner)

        @pl.when(c == 1)
        def _():
            put(4 + n, own.at[tail], prev.at[head], device_of(pos + 3))

    for n, (own, prev) in enumerate(pairs):
        sends.arrived(n, prev.at[mid], behind)

        @pl.when(c == 0)
        def _():
            put(4 + n, prev.at[pl.ds(rows, short)], prev.at[head], partner)

        @pl.when(c == 1)
        def _():
            put(2 + n, prev.at[mid], prev.at[end], partner)

    for n, (own, prev) in enumerate(pairs):
        sends.copy(2 + n, own, prev.at[end], partner).wait_send()
        sends.copy(4 + n, own.at[tail], prev.at[head], partner).wait_send()
        sends.arrived(2 + n, prev.at[end], partner)
        sends.arrived(4 + n, prev.at[head], partner)
    sends.drain()


def halo(k, v):
    width = k.shape[1]
    return pl.pallas_call(
        halo_kernel,
        out_shape=[jax.ShapeDtypeStruct((WIN, width), BF)] * 2,
        in_specs=[any_spec()] * 2,
        out_specs=[any_spec()] * 2,
        scratch_shapes=[pltpu.SemaphoreType.DMA((6,)), pltpu.SemaphoreType.DMA((6,))],
        compiler_params=pltpu.CompilerParams(
            collective_id=1, has_side_effects=True, vmem_limit_bytes=16 << 20
        ),
        name="halo",
    )(k, v)


def fine_kernel(
    x_ref, q_ref, k_ref, v_ref, kp_ref, vp_ref, w_ref, gain_ref,
    state_ref, pooled_ref, normed_ref,
    mix_ref, edge_out, edge_in, send_sem, recv_sem,
):
    rows = q_ref.shape[0]
    heads = q_ref.shape[1] // HE
    position = lax.axis_index("outer") * 16 + lax.axis_index("inner")
    greet([device_of(position + 1), device_of(position - 1)])
    t_prev = lax.broadcasted_iota(jnp.int32, (rows, WIN), 0)
    u_prev = lax.broadcasted_iota(jnp.int32, (rows, WIN), 1)
    ok_prev = (u_prev > t_prev) & (position * rows - WIN + u_prev >= 0)
    t_own = lax.broadcasted_iota(jnp.int32, (rows, rows), 0)
    u_own = lax.broadcasted_iota(jnp.int32, (rows, rows), 1)
    ok_own = u_own <= t_own
    for h in range(heads):
        cols = slice(h * HE, (h + 1) * HE)
        q = q_ref[:, cols]
        s_prev = lax.dot_general(q, kp_ref[:, cols], TRANS, preferred_element_type=F32) * SCALE
        s_own = lax.dot_general(q, k_ref[:, cols], TRANS, preferred_element_type=F32) * SCALE
        s_prev = jnp.where(ok_prev, s_prev, NEG)
        s_own = jnp.where(ok_own, s_own, NEG)
        top = jnp.maximum(
            jnp.max(s_prev, axis=-1, keepdims=True), jnp.max(s_own, axis=-1, keepdims=True)
        )
        p_prev = jnp.exp(s_prev - top)
        p_own = jnp.exp(s_own - top)
        total = jnp.sum(p_prev, axis=-1, keepdims=True) + jnp.sum(p_own, axis=-1, keepdims=True)
        mixed = jnp.dot(p_prev.astype(BF), vp_ref[:, cols], preferred_element_type=F32)
        mixed += jnp.dot(p_own.astype(BF), v_ref[:, cols], preferred_element_type=F32)
        mix_ref[:, cols] = (mixed / total).astype(BF)
    width = x_ref.shape[1]
    half = w_ref.shape[1]
    per = w_ref.shape[2]

    @pl.loop(0, NP // 2)
    def _(n):
        at = pl.ds(pl.multiple_of(n * per, per), per)
        prod = jnp.dot(mix_ref[:, :half], w_ref[n], preferred_element_type=F32)
        prod += jnp.dot(mix_ref[:, half:], w_ref[n + NP // 2], preferred_element_type=F32)
        state_ref[:, at] = (x_ref[:, at].astype(F32) + prod).astype(BF)

    edge_out[...] = state_ref[rows - POOL :, :]
    send = pltpu.make_async_remote_copy(
        src_ref=edge_out,
        dst_ref=edge_in,
        send_sem=send_sem,
        recv_sem=recv_sem,
        device_id=device_of(position + 1),
        device_id_type=MESH,
    )
    send.start()
    groups = state_ref[...].astype(F32).reshape(rows // POOL, POOL, width)
    first = groups[:, 0, :]
    rest = jnp.sum(groups[:, 1:, :], axis=1)
    send.wait()
    edge = jnp.sum(edge_in[...].astype(F32)[1:, :], axis=0, keepdims=True)
    edge = jnp.where(position == 0, 0.0, edge)
    before = jnp.concatenate([edge, rest[: rows // POOL - 1, :]], axis=0)
    pooled = ((before + first) / POOL).astype(BF)
    pooled_ref[...] = pooled
    wide = pooled.astype(F32)
    moment = jnp.mean(wide * wide, axis=-1, keepdims=True)
    normed_ref[...] = (wide * lax.rsqrt(moment + 1e-06) * gain_ref[...]).astype(BF)


def fine_stage(x, q, k, v, kp, vp, w, gain):
    rows, width = x.shape
    coarse = jax.ShapeDtypeStruct((rows // POOL, width), BF)
    return pl.pallas_call(
        fine_kernel,
        out_shape=[jax.ShapeDtypeStruct((rows, width), BF), coarse, coarse],
        in_specs=[vmem_spec()] * 8,
        out_specs=[vmem_spec()] * 3,
        scratch_shapes=[
            pltpu.VMEM(q.shape, BF),
            pltpu.VMEM((POOL, width), BF),
            pltpu.VMEM((POOL, width), BF),
            pltpu.SemaphoreType.DMA,
            pltpu.SemaphoreType.DMA,
        ],
        compiler_params=pltpu.CompilerParams(
            collective_id=2, has_side_effects=True, vmem_limit_bytes=40 << 20
        ),
        name="fine",
    )(x, q, k, v, kp, vp, w, gain.reshape(1, width))


ZCHUNK = 8


def z_gather_kernel(src_ref, dst_ref, local_sem, send_sem, recv_sem):
    x, y, z, c = place()
    up, down = device_at(x, y, (z + 1) % NZ, c), device_at(x, y, (z + NZ - 1) % NZ, c)
    greet([up, down])
    sends = Sends(send_sem, recv_sem)
    chunks = src_ref.shape[0] // ZCHUNK
    local = pltpu.make_async_copy(src_ref, dst_ref.at[z], local_sem)
    local.start()
    count_up, count_down = NZ // 2, NZ // 2 - 1
    for s in range(count_up + 1):
        for part in range(chunks):
            at = pl.ds(part * ZCHUNK, ZCHUNK)
            for sign, count, base, to, origin in (
                (-1, count_up, 0, up, down),
                (1, count_down, count_up * chunks, down, up),
            ):
                if s > count:
                    continue
                held = (z + sign * s + NZ) % NZ
                if s > 0:
                    sends.arrived(base + (s - 1) * chunks + part, dst_ref.at[held, at], origin)
                if s < count:
                    src = src_ref.at[at] if s == 0 else dst_ref.at[held, at]
                    sends.start(base + s * chunks + part, src, dst_ref.at[held, at], to)
    local.wait()
    sends.drain()


def gathered_along_z(block):
    chunks = block.shape[0] // ZCHUNK
    count = (NZ - 1) * chunks
    return pl.pallas_call(
        z_gather_kernel,
        out_shape=jax.ShapeDtypeStruct((NZ, *block.shape), block.dtype),
        in_specs=[any_spec()],
        out_specs=any_spec(),
        scratch_shapes=[
            pltpu.SemaphoreType.DMA,
            pltpu.SemaphoreType.DMA((count,)),
            pltpu.SemaphoreType.DMA((count,)),
        ],
        compiler_params=pltpu.CompilerParams(
            collective_id=3, has_side_effects=True, vmem_limit_bytes=16 << 20
        ),
        name="z_gather",
    )(block)


def z_exchange_kernel(src_ref, dst_ref, local_sem, send_sem, recv_sem):
    x, y, z, c = place()
    others = [device_at(x, y, (z + d) % NZ, c) for d in range(1, NZ)]
    greet(others)
    sends = Sends(send_sem, recv_sem)
    local = pltpu.make_async_copy(src_ref.at[z], dst_ref.at[z], local_sem)
    local.start()
    for d in (8, 7, 9, 6, 10, 5, 11, 4, 12, 3, 13, 2, 14, 1, 15):
        sends.start(d - 1, src_ref.at[(z + d) % NZ], dst_ref.at[z], others[d - 1])
    local.wait()
    for d in range(1, NZ):
        origin = (z + NZ - d) % NZ
        sends.arrived(d - 1, dst_ref.at[origin], device_at(x, y, origin, c))
    sends.drain()


def exchanged_along_z(blocks):
    return pl.pallas_call(
        z_exchange_kernel,
        out_shape=jax.ShapeDtypeStruct(blocks.shape, blocks.dtype),
        in_specs=[any_spec()],
        out_specs=any_spec(),
        scratch_shapes=[
            pltpu.SemaphoreType.DMA,
            pltpu.SemaphoreType.DMA((NZ - 1,)),
            pltpu.SemaphoreType.DMA((NZ - 1,)),
        ],
        compiler_params=pltpu.CompilerParams(
            collective_id=4, has_side_effects=True, vmem_limit_bytes=16 << 20
        ),
        name="z_exchange",
    )(blocks)


def scatter_kernel(src_ref, dst_ref, local_sem, send_sem, recv_sem):
    outer = lax.axis_index("outer")
    inner = lax.axis_index("inner")
    head = outer // 2
    others = [(outer, (inner + d) % 16) for d in range(1, 16)]
    greet(others)
    sends = Sends(send_sem, recv_sem)

    @pl.when(inner == head)
    def _():
        local = pltpu.make_async_copy(src_ref.at[inner], dst_ref, local_sem)
        local.start()
        for d in range(1, 16):
            to = (inner + d) % 16
            pltpu.make_async_remote_copy(
                src_ref=src_ref.at[to],
                dst_ref=dst_ref,
                send_sem=send_sem.at[d - 1],
                recv_sem=recv_sem,
                device_id=(outer, to),
                device_id_type=MESH,
            ).start()
        local.wait()
        for d in range(1, 16):
            pltpu.make_async_copy(src_ref.at[0], src_ref.at[0], send_sem.at[d - 1]).wait()

    @pl.when(inner != head)
    def _():
        pltpu.make_async_copy(dst_ref, dst_ref, recv_sem).wait()


def scattered_from_head(pieces):
    return pl.pallas_call(
        scatter_kernel,
        out_shape=jax.ShapeDtypeStruct(pieces.shape[1:], pieces.dtype),
        in_specs=[any_spec()],
        out_specs=any_spec(),
        scratch_shapes=[
            pltpu.SemaphoreType.DMA,
            pltpu.SemaphoreType.DMA((15,)),
            pltpu.SemaphoreType.DMA,
        ],
        compiler_params=pltpu.CompilerParams(
            collective_id=5, has_side_effects=True, vmem_limit_bytes=16 << 20
        ),
        name="scatter",
    )(pieces)


def coarse_kernel(q_ref, kv_ref, out_ref, top_ref, acc_ref):
    x, y, z, c = place()
    me = slot_of(x, y, c)
    count = q_ref.shape[0]
    per = count // NZ
    factor = SCALE * LOG2E
    top_ref[...] = jnp.full(top_ref.shape, NEG, F32)
    acc_ref[...] = jnp.zeros(acc_ref.shape, F32)
    ones = jnp.ones((count, HE), BF)
    t = lax.broadcasted_iota(jnp.int32, (count, count), 0)
    u = lax.broadcasted_iota(jnp.int32, (count, count), 1)
    t_plane, u_plane = t // per, u // per

    @pl.loop(0, NP)
    def _(d):
        s = lax.dot_general(
            q_ref[...], kv_ref[d, :, :HE], TRANS, preferred_element_type=F32
        ) * factor
        reach = jnp.where(d < me, t_plane * per + per - 1, jnp.where(d == me, t, t_plane * per - 1))
        s = jnp.where(u <= reach, s, NEG)
        old = top_ref[...]
        new = jnp.maximum(old, jnp.max(s, axis=-1, keepdims=True))
        p = jnp.where(u <= reach, jnp.exp2(s - new), 0.0).astype(BF)
        wide = jnp.concatenate([kv_ref[d, :, HE:], ones], axis=1)
        acc_ref[...] = acc_ref[...] * jnp.exp2(old - new) + jnp.dot(
            p, wide, preferred_element_type=F32
        )
        top_ref[...] = new

    out_ref[...] = (acc_ref[:, :HE] / acc_ref[:, HE:]).astype(BF)


def coarse_stage(q, kv):
    return pl.pallas_call(
        coarse_kernel,
        out_shape=jax.ShapeDtypeStruct(q.shape, BF),
        in_specs=[vmem_spec()] * 2,
        out_specs=vmem_spec(),
        scratch_shapes=[
            pltpu.VMEM((q.shape[0], 1), F32),
            pltpu.VMEM((q.shape[0], 2 * HE), F32),
        ],
        compiler_params=pltpu.CompilerParams(vmem_limit_bytes=40 << 20),
        name="coarse",
    )(q, kv)


def on_device(
    fine_input,
    fine_query,
    fine_key,
    fine_value,
    w_fine_out,
    norm_gain,
    w_query,
    w_key,
    w_value,
    w_coarse_out,
):
    rows, width = fine_input.shape
    copy = lax.axis_index("outer") % 2

    def half_of(w):
        size = w.shape[0] // 2
        return lax.dynamic_slice_in_dim(w, copy * size, size, 0)

    kp, vp = halo(fine_key, fine_value)
    w_fine = gathered_in_plane(half_of(w_fine_out), 6)
    w_out = gathered_in_plane(half_of(w_coarse_out), 7)
    joined = jnp.concatenate([w_query, w_key, w_value], axis=1)
    head_width = joined.shape[1]
    piece = scattered_from_head(half_of(joined).reshape(16, -1, head_width))
    w_head = gathered_in_plane(piece, 8).reshape(width, head_width)
    state, pooled, normed = fine_stage(
        fine_input, fine_query, fine_key, fine_value, kp, vp, w_fine, norm_gain
    )
    tokens = gathered_along_z(normed).reshape(-1, width)
    proj = jnp.dot(tokens, w_head, preferred_element_type=F32).astype(BF)
    kv = gathered_in_plane(proj[:, HE:], 9)
    mix = coarse_stage(proj[:, :HE], kv)
    heads = exchanged_along_z(mix.reshape(NZ, -1, HE))
    heads = heads.reshape(NZ, rows // POOL, 2, HE // 2).transpose(1, 2, 0, 3)
    head_total = jnp.dot(
        heads.reshape(rows // POOL, -1), w_out.reshape(-1, width), preferred_element_type=F32
    )
    coarse_out = (pooled.astype(F32) + head_total).astype(BF)
    groups = state.reshape(rows // POOL, POOL, width).astype(F32)
    lifted = groups + coarse_out.astype(F32)[:, None, :]
    return lifted.reshape(rows, width).astype(BF)


def solution(mesh):
    placed = (
        P(("outer", "inner"), None),
        P(("outer", "inner"), None),
        P(("outer", "inner"), None),
        P(("outer", "inner"), None),
        P(None, "inner"),
        P(),
        P(None, "inner"),
        P(None, "inner"),
        P(None, "inner"),
        P("inner", None),
    )
    return jax.shard_map(
        on_device,
        mesh=mesh,
        in_specs=placed,
        out_specs=P(("outer", "inner"), None),
        check_vma=False,
    )
```

time: 393 us -> 242 us (0.62)
  Pallas kernels: 0 us -> 236 us
  waiting for transfers between devices: 231 us -> 0 us
  blocking collectives: 69.9 us -> 0 us
  matrix products: 32.6 us -> 2.19 us
  starting transfers between devices: 22.9 us -> 0 us
  other arithmetic: 18.8 us -> 2.29 us
  between operations: 13.6 us -> 0.21 us
    pallas_call x0 -> x10, Pallas kernels: none -> 236 us  [the longest x4 108 us: gathered_in_plane(): pl.pallas_call(gather_kernel, out_shape=jax.ShapeDtypeStruct((NP, *block....]
    all_gather x2 -> x0, waiting for transfers between devices: 173 us -> none  [the longest x1 173 us: sent_together(): out, at, outs = (lax.all_gather(both, axis, axis=dim, tiled=True), 0, [])]
    all_to_all x2 -> x0, blocking collectives: 69.9 us -> none  [the longest x1 36.4 us: copy_for_each(): return lax.all_to_all(copies, axis, split_axis=0, concat_axis=0, tiled=True)]
    ppermute x7 -> x0, waiting for transfers between devices: 56.7 us -> none  [passed_along(): return lax.ppermute(block, axis, route)]
    dot_general x6 -> x2, matrix products: 26.8 us -> 2.19 us  [the longest x1 1.21 us: on_device(): jnp.dot(heads.reshape(rows // POOL, -1), w_out.reshape(-1, width), prefer...]
    ppermute x7 -> x0, starting transfers between devices: 22.9 us -> none  [passed_along(): return lax.ppermute(block, axis, route)]
    reduce_sum x5 -> x0, other arithmetic: 12.1 us -> none  [the longest x1 11.1 us: attend(): new_sum = jnp.sum(block_exp, axis=-1)]
    sub x1 -> x0, matrix products: 5.81 us -> none  [on_device(): exp_weights = jnp.where(allowed[None], jnp.exp(scores - row_max), 0.0)]
  transfers between devices with their start and end apart: 9 -> 0, of which waited for: 6 -> 0; matrix products, arithmetic and copies ran while one was open for 4% -> 0% of each run, Pallas kernels for 0% -> 0%
where the time goes in v1:
time: 242 us
  Pallas kernels  236 us (98%)
    pallas_call x4, Pallas kernels, gathered_in_plane(): pl.pallas_call(gather_kernel, out_shape=jax.ShapeDtypeStruct((NP, *block....  108 us
    pallas_call x1, Pallas kernels, halo(): pl.pallas_call(halo_kernel, out_shape=[jax.ShapeDtypeStruct((WIN, width),...  37.3 us
    pallas_call x1, Pallas kernels, gathered_along_z(): pl.pallas_call(z_gather_kernel, out_shape=jax.ShapeDtypeStruct((NZ, *bloc...  27.5 us
    pallas_call x1, Pallas kernels, coarse_stage(): pl.pallas_call(coarse_kernel, out_shape=jax.ShapeDtypeStruct(q.shape, BF)...  24.7 us
    pallas_call x1, Pallas kernels, fine_stage(): pl.pallas_call(fine_kernel, out_shape=[jax.ShapeDtypeStruct((rows, width)...  14.9 us
    pallas_call x1, Pallas kernels, exchanged_along_z(): pl.pallas_call(z_exchange_kernel, out_shape=jax.ShapeDtypeStruct(blocks.s...  14.6 us
    pallas_call x1, Pallas kernels, scattered_from_head(): pl.pallas_call(scatter_kernel, out_shape=jax.ShapeDtypeStruct(pieces.shap...  8.8 us

profile of v1, /device:TPU:1, one launch (start us, length us, event | category | flops | bytes accessed | tf_op | source)
XLA Modules:
  0.0 241.8 jit_solution(15107993162385144220)
XLA Ops:
  0.0 0.0 copy-start
  0.0 1.0 constant_dynamic-slice_fusion.1.src_ref
  1.0 0.1 copy-done
  1.1 1.2 fusion.4
  2.4 0.0 copy-start.1
  2.4 0.0 copy-start.2
  2.4 8.8 %scatter.1.src_ref = bf16[64,384]{1,0:T(8,128)(2,1)S(1)} custom-call(bf16[16,64,384]{2,1,0:T(8,128)(2,1)S(1)} %bitcast.20), custom_call_target="tpu_custom_call" | custom-call | tf_op jit(solution)/shard_map/scatter/pallas_call | solution.py:546
  11.2 22.6 %plane_gather_8.1 = bf16[32,64,384]{2,1,0:T(8,128)(2,1)S(1)} custom-call(bf16[64,384]{1,0:T(8,128)(2,1)S(1)} %scatter.1.src_ref), custom_call_target="tpu_custom_call" | custom-call | tf_op jit(solution)/shard_map/plane_gather_8/pallas_call | solution.py:262
  33.8 0.0 copy-done.1
  33.8 0.0 copy-done.2
  33.8 37.3 %halo.1 = (bf16[512,1024]{1,0:T(8,128)(2,1)S(1)}, bf16[512,1024]{1,0:T(8,128)(2,1)S(1)}) custom-call(bf16[192,1024]{1,0:T(8,128)(2,1)S(1)} %copy-done.1, bf16[192,1024]{1,0:T(8,128)(2,1)S(1)} %copy-done.2), custom_call_target="tpu_custom_call" | custom-call | tf_op jit(solution)/shard_map/halo/pallas_call | solution.py:328
  71.1 0.0 copy-start.3
  71.1 0.0 copy-start.4
  71.1 0.0 copy-start.5
  71.2 22.4 %plane_gather_6.1.w_ref = bf16[32,512,128]{2,1,0:T(8,128)(2,1)S(1)} custom-call(bf16[512,128]{1,0:T(8,128)(2,1)S(1)} %constant_dynamic-slice_fusion.1.src_ref), custom_call_target="tpu_custom_call" | custom-call | tf_op jit(solution)/shard_map/plane_gather_6/pallas_call | solution.py:262
  93.5 0.0 copy-done.3
  93.5 0.0 copy-done.4
  93.6 0.0 copy-done.5
  93.6 14.9 %fine.1 = (bf16[192,2048]{1,0:T(8,128)(2,1)S(1)}, bf16[24,2048]{1,0:T(8,128)(2,1)S(1)}, bf16[24,2048]{1,0:T(8,128)(2,1)S(1)}) custom-call(bf16[192,2048]{1,0:T(8,128)(2,1)S(1)} %copy-done.3, bf16[192,1024]{1,0:T(8,128)(2,1)S(1)} %copy-done.4, bf16[192,1024]{1,0:T(8,128)(2,1)S(1)} %copy-done.1, bf16[192,1024]{1,0:T(8,128)(2,1)S(1)} %copy-done.2, ...), custom_call_target="tpu_custom_call" | custom-call | tf_op jit(solution)/shard_map/fine/pallas_call | solution.py:410
  108.4 27.5 %z_gather.1 = bf16[16,24,2048]{2,1,0:T(8,128)(2,1)S(1)} custom-call(bf16[24,2048]{1,0:T(8,128)(2,1)S(1)} %get-tuple-element.14.src_ref), custom_call_target="tpu_custom_call" | custom-call | tf_op jit(solution)/shard_map/z_gather/pallas_call | solution.py:463
  136.0 1.0 convolution_convert_fusion
  137.0 31.8 %plane_gather_9.1.kv_ref = bf16[32,384,256]{2,1,0:T(8,128)(2,1)S(1)} custom-call(bf16[384,256]{1,0:T(8,128)(2,1)S(1)} %slice.9.src_ref), custom_call_target="tpu_custom_call" | custom-call | tf_op jit(solution)/shard_map/plane_gather_9/pallas_call | solution.py:262
  168.8 24.7 %coarse.1 = bf16[384,128]{1,0:T(8,128)(2,1)S(1)} custom-call(bf16[384,128]{1,0:T(8,128)(2,1)S(1)} %slice.8.q_ref, bf16[32,384,256]{2,1,0:T(8,128)(2,1)S(1)} %plane_gather_9.1.kv_ref), custom_call_target="tpu_custom_call" | custom-call | tf_op jit(solution)/shard_map/coarse/pallas_call | solution.py:596
  193.5 14.6 %z_exchange.1 = bf16[16,24,128]{2,1,0:T(8,128)(2,1)S(1)} custom-call(bf16[16,24,128]{2,1,0:T(8,128)(2,1)S(1)} %bitcast.23), custom_call_target="tpu_custom_call" | custom-call | tf_op jit(solution)/shard_map/z_exchange/pallas_call | solution.py:497
  208.1 0.1 reshape.33
  208.3 0.1 copy.13
  208.3 0.2 reshape.34
  208.6 30.9 %plane_gather_7.1 = bf16[32,64,2048]{2,1,0:T(8,128)(2,1)S(1)} custom-call(bf16[64,2048]{1,0:T(8,128)(2,1)S(1)} %constant_dynamic-slice_fusion.src_ref), custom_call_target="tpu_custom_call" | custom-call | tf_op jit(solution)/shard_map/plane_gather_7/pallas_call | solution.py:262
  239.5 1.2 fusion.1
  240.7 1.1 fusion.2
  (3 shorter events, 0.0 us)
Async XLA Ops:
  0.0 1.1 copy-start
  2.4 31.5 %copy-start.1 = (bf16[192,1024]{1,0:T(8,128)(2,1)S(1)}, bf16[192,1024]{1,0:T(8,128)(2,1)}, u32[]{:S(2)}) copy-start(bf16[192,1024]{1,0:T(8,128)(2,1)} %k_ref.3) | copy-start | bytes 1179652
  2.4 31.5 %copy-start.2 = (bf16[192,1024]{1,0:T(8,128)(2,1)S(1)}, bf16[192,1024]{1,0:T(8,128)(2,1)}, u32[]{:S(2)}) copy-start(bf16[192,1024]{1,0:T(8,128)(2,1)} %v_ref.3) | copy-start | bytes 1179652
  71.1 22.4 %copy-start.3 = (bf16[192,2048]{1,0:T(8,128)(2,1)S(1)}, bf16[192,2048]{1,0:T(8,128)(2,1)}, u32[]{:S(2)}) copy-start(bf16[192,2048]{1,0:T(8,128)(2,1)} %x_ref.1) | copy-start | bytes 2359300
  71.1 22.4 %copy-start.4 = (bf16[192,1024]{1,0:T(8,128)(2,1)S(1)}, bf16[192,1024]{1,0:T(8,128)(2,1)}, u32[]{:S(2)}) copy-start(bf16[192,1024]{1,0:T(8,128)(2,1)} %q_ref.1) | copy-start | bytes 1179652
  71.1 22.4 %copy-start.5 = (f32[2048]{0:T(1024)S(1)}, f32[2048]{0:T(1024)}, u32[]{:S(2)}) copy-start(f32[2048]{0:T(1024)} %param.15) | copy-start | bytes 24580

commit v2 on v1

v2 whole, which is shorter than its diff:
```python
import functools
import math

import jax
import jax.numpy as jnp
from jax import lax
from jax.experimental import pallas as pl
from jax.experimental.pallas import tpu as pltpu
from jax.sharding import PartitionSpec as P

HE = 128
WIN = 512
POOL = 8
NEG = -1e30
LOG2E = math.log2(math.e)
SCALE = 1.0 / math.sqrt(HE)
BF = jnp.bfloat16
F32 = jnp.float32
TRANS = (((1,), (1,)), ((), ()))
MESH = pl.DeviceIdType.MESH
NX, NY, NZ, NC = 4, 4, 16, 2
NP = NX * NY * NC


def vmem_spec():
    return pl.BlockSpec(memory_space=pltpu.VMEM)


def any_spec():
    return pl.BlockSpec(memory_space=pl.ANY)


def place():
    outer = lax.axis_index("outer")
    inner = lax.axis_index("inner")
    x = (outer % 2) * 2 + inner // 8
    return x, (inner // 2) % NY, outer // 2, inner % NC


def device_at(x, y, z, c):
    return (z * 2 + x // 2, (x % 2) * 8 + y * 2 + c)


def device_of(pos):
    pos = (pos + 512) % 512
    return (pos // 16, pos % 16)


def slot_of(x, y, c):
    return x * 8 + y * 2 + c


def greet(devices):
    barrier = pltpu.get_barrier_semaphore()
    for d in devices:
        pl.semaphore_signal(barrier, inc=1, device_id=d, device_id_type=MESH)
    pl.semaphore_wait(barrier, len(devices))


def plane_neighbours():
    x, y, z, c = place()
    return [
        device_at((x + 1) % NX, y, z, c),
        device_at((x + 3) % NX, y, z, c),
        device_at(x, (y + 1) % NY, z, c),
        device_at(x, (y + 3) % NY, z, c),
        device_at(x, y, z, 1 - c),
    ]


class Sends:
    def __init__(self, send_sem, recv_sem, base=0):
        self.send_sem, self.recv_sem, self.next = send_sem, recv_sem, base
        self.started = []

    def new(self):
        self.next += 1
        return self.next - 1

    def copy(self, k, src, dst, to):
        return pltpu.make_async_remote_copy(
            src_ref=src,
            dst_ref=dst,
            send_sem=self.send_sem.at[k],
            recv_sem=self.recv_sem.at[k],
            device_id=to,
            device_id_type=MESH,
        )

    def start(self, k, src, dst, to):
        c = self.copy(k, src, dst, to)
        c.start()
        self.started.append(c)

    def arrived(self, k, dst, to):
        self.copy(k, dst, dst, to).wait_recv()

    def drain(self):
        for c in self.started:
            c.wait_send()
        self.started = []


def plane_copies(firsts):
    return 35 * len(firsts) + 1


def plane_gather(sends, src, dst, local_sem, firsts=(0, 1)):
    x, y, z, c = place()
    part = src.shape[0] // len(firsts)

    def near(axis, off):
        if axis == 0:
            return device_at((x + off) % NX, y, z, c)
        return device_at(x, (y + off) % NY, z, c)

    def at(axis, a, b):
        if axis == 0:
            return slot_of((x + a) % NX, (y + b) % NY, c)
        return slot_of((x + b) % NX, (y + a) % NY, c)

    partner = device_at(x, y, z, 1 - c)
    halves = []
    for n, first in enumerate(firsts):
        lo = n * part
        h = dict(first=first, whole=pl.ds(lo, part), k={})
        h["q0"] = pl.ds(lo, part // 2)
        h["q1"] = pl.ds(lo + part // 2, part // 2)
        for name in ("r1", "l1", "r2", "l2"):
            h["k"][name] = sends.new()
        for j in (0, -1, 1, 2):
            for name in ("r1", "l1", "r2", "l2"):
                h["k"][name, j] = sends.new()
        for j in (0, -1, 1, 2):
            for i in (0, -1, 1, 2):
                if (i, j) != (0, 0):
                    h["k"]["p", j, i] = sends.new()
        halves.append(h)
    own_pair = sends.new()
    mine = slot_of(x, y, c)
    theirs = slot_of(x, y, 1 - c)
    local = pltpu.make_async_copy(src, dst.at[mine], local_sem)

    def to_partner(h, j, i):
        s = at(h["first"], j, i)
        sends.start(h["k"]["p", j, i], dst.at[s, h["whole"]], dst.at[s, h["whole"]], partner)

    for second_axis in (False, True):
        for h in halves:
            a = 1 - h["first"] if second_axis else h["first"]
            for name, off in (("r1", 1), ("l1", -1)):
                k = h["k"][(name, 0) if second_axis else name]
                sends.start(k, src.at[h["whole"]], dst.at[mine, h["whole"]], near(a, off % 4))
    sends.start(own_pair, src, dst.at[mine], partner)
    local.start()
    yield

    def second(h, j):
        s = at(h["first"], j, 0)
        for name, off in (("r1", 1), ("l1", -1)):
            sends.start(
                h["k"][name, j],
                dst.at[s, h["whole"]],
                dst.at[s, h["whole"]],
                near(1 - h["first"], off % 4),
            )
        to_partner(h, j, 0)

    directions = (("r1", "r2", -1, "q0"), ("l1", "l2", 1, "q1"))
    for h in halves:
        a = h["first"]
        for name, fwd, off, q in directions:
            s = at(a, off, 0)
            sends.arrived(h["k"][name], dst.at[s, h["whole"]], near(a, off % 4))
            sends.start(h["k"][fwd], dst.at[s, h[q]], dst.at[s, h[q]], near(a, (-off) % 4))
    for h in halves:
        for off in (-1, 1):
            second(h, off)
    yield

    def relay(h, j):
        b = 1 - h["first"]
        for name, fwd, off, q in directions:
            s = at(h["first"], j, off)
            sends.arrived(h["k"][name, j], dst.at[s, h["whole"]], near(b, off % 4))
            sends.start(h["k"][fwd, j], dst.at[s, h[q]], dst.at[s, h[q]], near(b, (-off) % 4))
            to_partner(h, j, off)

    for h in halves:
        relay(h, 0)
    yield
    for h in halves:
        a = h["first"]
        s = at(a, 2, 0)
        sends.arrived(h["k"]["r2"], dst.at[s, h["q0"]], near(a, 3))
        sends.arrived(h["k"]["l2"], dst.at[s, h["q1"]], near(a, 1))
        second(h, 2)
    yield

    def last(h, j):
        b = 1 - h["first"]
        s = at(h["first"], j, 2)
        sends.arrived(h["k"]["r2", j], dst.at[s, h["q0"]], near(b, 3))
        sends.arrived(h["k"]["l2", j], dst.at[s, h["q1"]], near(b, 1))
        to_partner(h, j, 2)

    for j in (-1, 1):
        for h in halves:
            relay(h, j)
    for h in halves:
        last(h, 0)
    yield
    for h in halves:
        relay(h, 2)
    for j in (-1, 1):
        for h in halves:
            last(h, j)
    yield
    for h in halves:
        last(h, 2)
    local.wait()
    sends.arrived(own_pair, dst.at[theirs], partner)
    for h in halves:
        for j in (0, -1, 1, 2):
            for i in (0, -1, 1, 2):
                if (i, j) != (0, 0):
                    s = at(h["first"], j, i) + 1 - 2 * c
                    sends.arrived(h["k"]["p", j, i], dst.at[s, h["whole"]], partner)
    yield


def run_all(steps):
    for _ in steps:
        pass


HALO_COPIES = 8
W_FIRSTS = (1,)


def halo_copies(sends, k_ref, v_ref, kp_ref, vp_ref, relay_ref):
    x, y, z, c = place()
    pos = lax.axis_index("outer") * 16 + lax.axis_index("inner")
    rows = k_ref.shape[0]
    short = WIN - 2 * rows
    ahead, behind = device_of(pos + 2), device_of(pos - 2)
    partner = device_at(x, y, z, 1 - c)
    down, up = device_at(x, (y + 3) % NY, z, c), device_at(x, (y + 1) % NY, z, c)
    relay_to = relay_target()
    pairs = ((k_ref, kp_ref), (v_ref, vp_ref))
    mid, end = pl.ds(short, rows), pl.ds(short + rows, rows)
    head, tail = pl.ds(0, short), pl.ds(rows - short, short)

    def put(n, src, dst, to):
        sends.copy(n, src, dst, to).start()

    for n, (own, prev) in enumerate(pairs):
        put(n, own, prev.at[mid], ahead)

        @pl.when(c == 0)
        def _():
            put(2 + n, own, prev.at[end], partner)

        @pl.when(c == 1)
        def _():
            put(6 + n, own.at[tail], relay_ref.at[n], down)

        yield

    for n, (own, prev) in enumerate(pairs):

        @pl.when(c == 1)
        def _():
            sends.copy(6 + n, relay_ref.at[n], relay_ref.at[n], up).wait_recv()
            put(4 + n, relay_ref.at[n], prev.at[head], relay_to)

        yield
    for n, (own, prev) in enumerate(pairs):
        sends.arrived(n, prev.at[mid], behind)

        @pl.when(c == 0)
        def _():
            put(4 + n, prev.at[pl.ds(rows, short)], prev.at[head], partner)

        @pl.when(c == 1)
        def _():
            put(2 + n, prev.at[mid], prev.at[end], partner)

        yield
    for n, (own, prev) in enumerate(pairs):
        sends.arrived(2 + n, prev.at[end], partner)
        sends.arrived(4 + n, prev.at[head], partner)
        sends.copy(n, own, prev.at[mid], ahead).wait_send()
        sends.copy(2 + n, own, prev.at[end], partner).wait_send()
        sends.copy(4 + n, own.at[tail], prev.at[head], partner).wait_send()

        @pl.when(c == 1)
        def _():
            sends.copy(6 + n, own.at[tail], relay_ref.at[n], down).wait_send()

    yield


def relay_target():
    x, y, z, c = place()
    pos = lax.axis_index("outer") * 16 + lax.axis_index("inner")
    above_o, above_i = device_at(x, (y + 1) % NY, z, 1)
    to_o, to_i = device_of(above_o * 16 + above_i + 3)
    from_o, from_i = device_of(pos - 3)
    fx, fy, fz = (from_o % 2) * 2 + from_i // 8, (from_i // 2) % NY, from_o // 2
    by_o, by_i = device_at(fx, (fy + 3) % NY, fz, 1)
    return jnp.where(c == 1, to_o, by_o), jnp.where(c == 1, to_i, by_i)


def fine_kernel(
    x_ref, q_ref, k_ref, v_ref, w_src, gain_ref,
    state_ref, pooled_ref, normed_ref,
    mix_ref, edge_out, edge_in, kp_ref, vp_ref, relay_ref, w_ref, local_sem, send_sem, recv_sem,
):
    rows = q_ref.shape[0]
    heads = q_ref.shape[1] // HE
    position = lax.axis_index("outer") * 16 + lax.axis_index("inner")
    greet(
        plane_neighbours()
        + [device_of(position + d) for d in (2, -2, 1, -1)]
        + [relay_target()]
    )
    sends = Sends(send_sem, recv_sem, HALO_COPIES)
    weights = plane_gather(sends, w_src, w_ref, local_sem, W_FIRSTS)
    rows_before = halo_copies(sends, k_ref, v_ref, kp_ref, vp_ref, relay_ref)
    next(weights)
    next(rows_before)
    next(weights)
    next(rows_before)
    next(weights)
    run_all(rows_before)
    next(weights)
    t_prev = lax.broadcasted_iota(jnp.int32, (rows, WIN), 0)
    u_prev = lax.broadcasted_iota(jnp.int32, (rows, WIN), 1)
    ok_prev = (u_prev > t_prev) & (position * rows - WIN + u_prev >= 0)
    t_own = lax.broadcasted_iota(jnp.int32, (rows, rows), 0)
    u_own = lax.broadcasted_iota(jnp.int32, (rows, rows), 1)
    ok_own = u_own <= t_own
    for h in range(heads):
        cols = slice(h * HE, (h + 1) * HE)
        q = q_ref[:, cols]
        s_prev = lax.dot_general(q, kp_ref[:, cols], TRANS, preferred_element_type=F32) * SCALE
        s_own = lax.dot_general(q, k_ref[:, cols], TRANS, preferred_element_type=F32) * SCALE
        s_prev = jnp.where(ok_prev, s_prev, NEG)
        s_own = jnp.where(ok_own, s_own, NEG)
        top = jnp.maximum(
            jnp.max(s_prev, axis=-1, keepdims=True), jnp.max(s_own, axis=-1, keepdims=True)
        )
        p_prev = jnp.exp(s_prev - top)
        p_own = jnp.exp(s_own - top)
        total = jnp.sum(p_prev, axis=-1, keepdims=True) + jnp.sum(p_own, axis=-1, keepdims=True)
        mixed = jnp.dot(p_prev.astype(BF), vp_ref[:, cols], preferred_element_type=F32)
        mixed += jnp.dot(p_own.astype(BF), v_ref[:, cols], preferred_element_type=F32)
        mix_ref[:, cols] = (mixed / total).astype(BF)
        if h in (1, 3):
            next(weights)
    run_all(weights)
    width = x_ref.shape[1]
    half = w_ref.shape[1]
    per = w_ref.shape[2]

    @pl.loop(0, NP // 2)
    def _(n):
        at = pl.ds(pl.multiple_of(n * per, per), per)
        prod = jnp.dot(mix_ref[:, :half], w_ref[n], preferred_element_type=F32)
        prod += jnp.dot(mix_ref[:, half:], w_ref[n + NP // 2], preferred_element_type=F32)
        state_ref[:, at] = (x_ref[:, at].astype(F32) + prod).astype(BF)

    edge_out[...] = state_ref[rows - POOL :, :]
    send = pltpu.make_async_remote_copy(
        src_ref=edge_out,
        dst_ref=edge_in,
        send_sem=send_sem.at[EDGE_COPY],
        recv_sem=recv_sem.at[EDGE_COPY],
        device_id=device_of(position + 1),
        device_id_type=MESH,
    )
    send.start()
    groups = state_ref[...].astype(F32).reshape(rows // POOL, POOL, width)
    first = groups[:, 0, :]
    rest = jnp.sum(groups[:, 1:, :], axis=1)
    send.wait()
    edge = jnp.sum(edge_in[...].astype(F32)[1:, :], axis=0, keepdims=True)
    edge = jnp.where(position == 0, 0.0, edge)
    before = jnp.concatenate([edge, rest[: rows // POOL - 1, :]], axis=0)
    pooled = ((before + first) / POOL).astype(BF)
    pooled_ref[...] = pooled
    wide = pooled.astype(F32)
    moment = jnp.mean(wide * wide, axis=-1, keepdims=True)
    normed_ref[...] = (wide * lax.rsqrt(moment + 1e-06) * gain_ref[...]).astype(BF)
    sends.drain()


EDGE_COPY = HALO_COPIES + plane_copies(W_FIRSTS)


def fine_stage(x, q, k, v, w_half, gain):
    rows, width = x.shape
    coarse = jax.ShapeDtypeStruct((rows // POOL, width), BF)
    return pl.pallas_call(
        fine_kernel,
        out_shape=[jax.ShapeDtypeStruct((rows, width), BF), coarse, coarse],
        in_specs=[vmem_spec()] * 6,
        out_specs=[vmem_spec()] * 3,
        scratch_shapes=[
            pltpu.VMEM(q.shape, BF),
            pltpu.VMEM((POOL, width), BF),
            pltpu.VMEM((POOL, width), BF),
            pltpu.VMEM((WIN, k.shape[1]), BF),
            pltpu.VMEM((WIN, k.shape[1]), BF),
            pltpu.VMEM((2, WIN - 2 * rows, k.shape[1]), BF),
            pltpu.VMEM((NP, *w_half.shape), BF),
            pltpu.SemaphoreType.DMA,
            pltpu.SemaphoreType.DMA((EDGE_COPY + 1,)),
            pltpu.SemaphoreType.DMA((EDGE_COPY + 1,)),
        ],
        compiler_params=pltpu.CompilerParams(
            collective_id=2, has_side_effects=True, vmem_limit_bytes=40 << 20
        ),
        name="fine",
    )(x, q, k, v, w_half, gain.reshape(1, width))


ZCHUNK = 8
HEAD_FIRSTS = (0, 1)


def z_copies(rows):
    return (NZ - 1) * (rows // ZCHUNK)


def z_gather(sends, src_ref, dst_ref, local_sem):
    x, y, z, c = place()
    up, down = device_at(x, y, (z + 1) % NZ, c), device_at(x, y, (z + NZ - 1) % NZ, c)
    chunks = src_ref.shape[0] // ZCHUNK
    first = sends.next
    sends.next += z_copies(src_ref.shape[0])
    count_up, count_down = NZ // 2, NZ // 2 - 1
    local = pltpu.make_async_copy(src_ref, dst_ref.at[z], local_sem)
    for s in range(count_up + 1):
        for part in range(chunks):
            at = pl.ds(part * ZCHUNK, ZCHUNK)
            for sign, count, base, to, origin in (
                (-1, count_up, first, up, down),
                (1, count_down, first + count_up * chunks, down, up),
            ):
                if s > count:
                    continue
                held = (z + sign * s + NZ) % NZ
                if s > 0:
                    sends.arrived(base + (s - 1) * chunks + part, dst_ref.at[held, at], origin)
                if s < count:
                    src = src_ref.at[at] if s == 0 else dst_ref.at[held, at]
                    sends.start(base + s * chunks + part, src, dst_ref.at[held, at], to)
        if s == 0:
            local.start()
        if s == count_up:
            local.wait()
        yield


def scatter(src_ref, dst_ref, local_sem, send_sem, recv_sem):
    outer = lax.axis_index("outer")
    inner = lax.axis_index("inner")
    head = outer // 2

    @pl.when(inner == head)
    def _():
        pltpu.make_async_copy(src_ref.at[inner], dst_ref, local_sem).start()
        for d in range(1, 16):
            to = (inner + d) % 16
            pltpu.make_async_remote_copy(
                src_ref=src_ref.at[to],
                dst_ref=dst_ref,
                send_sem=send_sem.at[d - 1],
                recv_sem=recv_sem,
                device_id=(outer, to),
                device_id_type=MESH,
            ).start()

    yield

    @pl.when(inner == head)
    def _():
        pltpu.make_async_copy(src_ref.at[inner], dst_ref, local_sem).wait()
        for d in range(1, 16):
            pltpu.make_async_copy(src_ref.at[0], src_ref.at[0], send_sem.at[d - 1]).wait()

    @pl.when(inner != head)
    def _():
        pltpu.make_async_copy(dst_ref, dst_ref, recv_sem).wait()

    yield


def middle_kernel(
    normed_ref, pieces_ref, w_src, tokens_ref, head_ref, w_ref,
    piece_ref, local_sem, scatter_send, scatter_recv, send_sem, recv_sem,
):
    x, y, z, c = place()
    outer = lax.axis_index("outer")
    inner = lax.axis_index("inner")
    ends = [device_at(x, y, (z + 1) % NZ, c), device_at(x, y, (z + NZ - 1) % NZ, c)]
    greet(plane_neighbours() + ends + [(outer, (inner + d) % 16) for d in range(1, 16)])
    sends = Sends(send_sem, recv_sem)
    along = z_gather(sends, normed_ref, tokens_ref, local_sem.at[0])
    pieces = scatter(pieces_ref, piece_ref, local_sem.at[1], scatter_send, scatter_recv)
    head = plane_gather(sends, piece_ref, head_ref, local_sem.at[2], HEAD_FIRSTS)
    out = plane_gather(sends, w_src, w_ref, local_sem.at[3])
    next(along)
    next(pieces)
    next(out)
    next(along)
    next(along)
    next(pieces)
    next(head)
    next(out)
    next(along)
    next(head)
    next(out)
    next(along)
    next(head)
    next(out)
    next(along)
    next(head)
    next(out)
    next(along)
    next(head)
    next(out)
    next(along)
    next(head)
    next(along)
    run_all(head)
    run_all(out)
    sends.drain()


def middle_stage(normed, pieces, w_half):
    count = z_copies(normed.shape[0]) + plane_copies(HEAD_FIRSTS) + plane_copies((0, 1))
    return pl.pallas_call(
        middle_kernel,
        out_shape=[
            jax.ShapeDtypeStruct((NZ, *normed.shape), BF),
            jax.ShapeDtypeStruct((NP, *pieces.shape[1:]), BF),
            jax.ShapeDtypeStruct((NP, *w_half.shape), BF),
        ],
        in_specs=[any_spec()] * 3,
        out_specs=[any_spec()] * 3,
        scratch_shapes=[
            pltpu.VMEM(pieces.shape[1:], BF),
            pltpu.SemaphoreType.DMA((4,)),
            pltpu.SemaphoreType.DMA((15,)),
            pltpu.SemaphoreType.DMA,
            pltpu.SemaphoreType.DMA((count,)),
            pltpu.SemaphoreType.DMA((count,)),
        ],
        compiler_params=pltpu.CompilerParams(
            collective_id=3, has_side_effects=True, vmem_limit_bytes=16 << 20
        ),
        name="middle",
    )(normed, pieces, w_half)


KEY_GROUP = 8
PLANE_GROUP = 4


def coarse_kernel(
    proj_ref, out_ref,
    kv_ref, top_ref, acc_ref, mix_ref, heads_ref, local_sem, send_sem, recv_sem,
):
    x, y, z, c = place()
    others = [device_at(x, y, (z + d) % NZ, c) for d in range(1, NZ)]
    greet(plane_neighbours() + others)
    sends = Sends(send_sem, recv_sem, NZ - 1)
    run_all(plane_gather(sends, proj_ref.at[:, HE:], kv_ref, local_sem))
    me = slot_of(x, y, c)
    count = proj_ref.shape[0]
    per = count // NZ
    step = PLANE_GROUP * per
    factor = SCALE * LOG2E
    top_ref[...] = jnp.full(top_ref.shape, NEG, F32)
    acc_ref[...] = jnp.zeros(acc_ref.shape, F32)
    width = KEY_GROUP * step
    ones = jnp.ones((width, HE), BF)
    t = lax.broadcasted_iota(jnp.int32, (step, 1), 0)
    u = lax.broadcasted_iota(jnp.int32, (1, width), 1)
    t_order = (t // per * NP + me) * 32 + t % per
    u_order = (u % step // per * NP + u // step) * 32 + u % per

    @pl.loop(0, NP // KEY_GROUP)
    def _(g):
        some = pl.ds(g * KEY_GROUP, KEY_GROUP)
        allowed = u_order <= t_order - g * (KEY_GROUP * 32)
        for n in range(NZ // PLANE_GROUP):
            lo = n * step
            keys = kv_ref[some, lo : lo + step, :HE].reshape(width, HE)
            values = kv_ref[some, lo : lo + step, HE:].reshape(width, HE)
            s = lax.dot_general(
                proj_ref[lo:, :HE], keys, TRANS, preferred_element_type=F32
            ) * factor
            edge = jnp.where(allowed, s[:step], NEG)
            s = jnp.concatenate([edge, s[step:]], axis=0) if lo + step < count else edge
            old = top_ref[lo:, :]
            new = jnp.maximum(old, jnp.max(s, axis=-1, keepdims=True))
            p = jnp.exp2(s - new).astype(BF)
            wide = jnp.concatenate([values, ones], axis=1)
            acc_ref[lo:, :] = acc_ref[lo:, :] * jnp.exp2(old - new) + jnp.dot(
                p, wide, preferred_element_type=F32
            )
            top_ref[lo:, :] = new

    mix_ref[...] = (acc_ref[:, :HE] / acc_ref[:, HE:]).astype(BF).reshape(mix_ref.shape)
    for d in (8, 7, 9, 6, 10, 5, 11, 4, 12, 3, 13, 2, 14, 1, 15):
        sends.start(d - 1, mix_ref.at[(z + d) % NZ], heads_ref.at[z], others[d - 1])
    heads_ref[z] = mix_ref[z]
    for d in range(1, NZ):
        origin = (z + NZ - d) % NZ
        sends.arrived(d - 1, heads_ref.at[origin], others[NZ - d - 1])
    sends.drain()
    out_ref[...] = heads_ref[...]


def coarse_stage(proj):
    rows = proj.shape[0]
    count = NZ - 1 + plane_copies((0, 1))
    return pl.pallas_call(
        coarse_kernel,
        out_shape=jax.ShapeDtypeStruct((NZ, rows // NZ, HE), BF),
        in_specs=[vmem_spec()],
        out_specs=vmem_spec(),
        scratch_shapes=[
            pltpu.VMEM((NP, rows, 2 * HE), BF),
            pltpu.VMEM((rows, 1), F32),
            pltpu.VMEM((rows, 2 * HE), F32),
            pltpu.VMEM((NZ, rows // NZ, HE), BF),
            pltpu.VMEM((NZ, rows // NZ, HE), BF),
            pltpu.SemaphoreType.DMA,
            pltpu.SemaphoreType.DMA((count,)),
            pltpu.SemaphoreType.DMA((count,)),
        ],
        compiler_params=pltpu.CompilerParams(
            collective_id=4, has_side_effects=True, vmem_limit_bytes=40 << 20
        ),
        name="coarse",
    )(proj)


def on_device(
    fine_input,
    fine_query,
    fine_key,
    fine_value,
    w_fine_out,
    norm_gain,
    w_query,
    w_key,
    w_value,
    w_coarse_out,
):
    rows, width = fine_input.shape
    copy = lax.axis_index("outer") % 2

    def half_of(w):
        size = w.shape[0] // 2
        return lax.dynamic_slice_in_dim(w, copy * size, size, 0)

    state, pooled, normed = fine_stage(
        fine_input, fine_query, fine_key, fine_value, half_of(w_fine_out), norm_gain
    )
    joined = jnp.concatenate([half_of(w_query), half_of(w_key), half_of(w_value)], axis=1)
    pieces = joined.reshape(16, -1, joined.shape[1])
    tokens, w_head, w_out = middle_stage(normed, pieces, half_of(w_coarse_out))
    proj = jnp.dot(
        tokens.reshape(-1, width), w_head.reshape(width, -1), preferred_element_type=F32
    ).astype(BF)
    heads = coarse_stage(proj)
    heads = heads.reshape(NZ, rows // POOL, 2, HE // 2).transpose(1, 2, 0, 3)
    head_total = jnp.dot(
        heads.reshape(rows // POOL, -1), w_out.reshape(-1, width), preferred_element_type=F32
    )
    coarse_out = (pooled.astype(F32) + head_total).astype(BF)
    groups = state.reshape(rows // POOL, POOL, width).astype(F32)
    lifted = groups + coarse_out.astype(F32)[:, None, :]
    return lifted.reshape(rows, width).astype(BF)


def solution(mesh):
    placed = (
        P(("outer", "inner"), None),
        P(("outer", "inner"), None),
        P(("outer", "inner"), None),
        P(("outer", "inner"), None),
        P(None, "inner"),
        P(),
        P(None, "inner"),
        P(None, "inner"),
        P(None, "inner"),
        P("inner", None),
    )
    return jax.shard_map(
        on_device,
        mesh=mesh,
        in_specs=placed,
        out_specs=P(("outer", "inner"), None),
        check_vma=False,
    )
```

time: 242 us -> 167 us (0.69)
  Pallas kernels: 236 us -> 153 us
  local copies, waits for them, and re-layouts: 1.56 us -> 6.94 us
  matrix products: 2.19 us -> 5.55 us
    pallas_call x9 -> x2, Pallas kernels: 221 us -> 94.5 us  [the longest x1 50.5 us: middle_stage(): pl.pallas_call(middle_kernel, out_shape=[jax.ShapeDtypeStruct((NZ, *norme...]
    pallas_call x1, Pallas kernels: 14.9 us -> 58.2 us  [fine_stage(): pl.pallas_call(fine_kernel, out_shape=[jax.ShapeDtypeStruct((rows, width)...]
    dot_general x1, matrix products: 1.21 us -> 4.58 us  [on_device(): jnp.dot(heads.reshape(rows // POOL, -1), w_out.reshape(-1, width), prefer...]
    unnamed x12 -> x14, local copies, waits for them, and re-layouts: 0.16 us -> 3.38 us
where the time goes in v2:
time: 167 us
  Pallas kernels  153 us (92%)
  local copies, waits for them, and re-layouts  6.94 us (4%)
  matrix products  5.55 us (3%)
    pallas_call x1, Pallas kernels, fine_stage(): pl.pallas_call(fine_kernel, out_shape=[jax.ShapeDtypeStruct((rows, width)...  58.2 us
    pallas_call x1, Pallas kernels, middle_stage(): pl.pallas_call(middle_kernel, out_shape=[jax.ShapeDtypeStruct((NZ, *norme...  50.5 us
    pallas_call x1, Pallas kernels, coarse_stage(): pl.pallas_call(coarse_kernel, out_shape=jax.ShapeDtypeStruct((NZ, rows //...  44.1 us
    dot_general x1, matrix products, on_device(): jnp.dot(heads.reshape(rows // POOL, -1), w_out.reshape(-1, width), prefer...  4.58 us
    unnamed x14, local copies, waits for them, and re-layouts  3.38 us

profile of v2, /device:TPU:1, one launch (start us, length us, event | category | flops | bytes accessed | tf_op | source)
XLA Modules:
  0.0 166.6 jit_solution(4497874376276623117)
XLA Ops:
  0.0 0.0 copy-start
  0.0 1.0 constant_dynamic-slice_fusion.4.w_src
  1.0 0.1 copy-done
  1.1 0.0 copy-start.2
  1.1 0.0 copy-start.3
  1.2 0.0 copy-start.4
  1.2 0.0 copy-start.5
  1.2 0.0 copy-start.6
  1.2 1.1 constant_dynamic-slice_fusion.3
  2.3 1.1 constant_dynamic-slice_fusion.1
  3.4 0.1 pad_maximum_fusion
  3.5 0.0 copy-done.2
  3.5 0.0 copy-done.3
  3.5 0.0 copy-done.4
  3.5 0.0 copy-done.5
  3.5 0.0 copy-done.6
  3.5 58.2 %fine.1 = (bf16[192,2048]{1,0:T(8,128)(2,1)S(1)}, bf16[24,2048]{1,0:T(8,128)(2,1)S(1)}, bf16[24,2048]{1,0:T(8,128)(2,1)S(1)}) custom-call(bf16[192,2048]{1,0:T(8,128)(2,1)S(1)} %copy-done.2, bf16[192,1024]{1,0:T(8,128)(2,1)S(1)} %copy-done.3, bf16[192,1024]{1,0:T(8,128)(2,1)S(1)} %copy-done.4, bf16[192,1024]{1,0:T(8,128)(2,1)S(1)} %copy-done.5, ...), custom_call_target="tpu_custom_call" | custom-call | tf_op jit(solution)/shard_map/fine/pallas_call | solution.py:405
  61.8 50.5 %middle.1 = (bf16[16,24,2048]{2,1,0:T(8,128)(2,1)S(1)}, bf16[32,64,384]{2,1,0:T(8,128)(2,1)S(1)}, bf16[32,64,2048]{2,1,0:T(8,128)(2,1)S(1)}) custom-call(bf16[24,2048]{1,0:T(8,128)(2,1)S(1)} %get-tuple-element.13.normed_ref, bf16[16,64,384]{2,1,0:T(8,128)(2,1)S(1)} %bitcast.19, bf16[64,2048]{1,0:T(8,128)(2,1)S(1)} %constant_dynamic-slice_fusion.w_src), custom_call_target="tpu_custom_call" | custom-call | tf_op jit(solution)/shard_map/middle/pallas_call | solution.py:545
  112.2 0.0 copy-start.1
  112.2 3.2 %copy-done.1 = bf16[32,64,2048]{2,1,0:T(8,128)(2,1)} copy-done((bf16[32,64,2048]{2,1,0:T(8,128)(2,1)}, bf16[32,64,2048]{2,1,0:T(8,128)(2,1)S(1)}, u32[]{:S(2)}) %copy-start.1) | copy-done | bytes 8388632
  115.5 1.0 convolution_convert_fusion.proj_ref
  116.4 44.1 %coarse.1 = bf16[16,24,128]{2,1,0:T(8,128)(2,1)S(1)} custom-call(bf16[384,384]{1,0:T(8,128)(2,1)S(1)} %convolution_convert_fusion.proj_ref), custom_call_target="tpu_custom_call" | custom-call | tf_op jit(solution)/shard_map/coarse/pallas_call | solution.py:632
  160.5 0.1 reshape.29
  160.6 0.1 copy.13
  160.7 0.2 reshape.30
  160.9 4.6 %fusion.1 = f32[24,2048]{1,0:T(8,128)S(1)} fusion(bf16[24,2048]{1,0:T(8,128)(2,1)S(1)} %reshape.30, bf16[2048,2048]{1,0:T(8,128)(2,1)} %bitcast.18, bf16[24,2048]{1,0:T(8,128)(2,1)S(1)} %get-tuple-element.12), kind=kOutput, calls=%fused_computation.2 | convolution fusion | flops 201523200 | bytes 8781824 | tf_op jit(solution)/shard_map/dot_general | solution.py:684
  165.5 1.1 fusion.2
  (1 shorter events, 0.0 us)
Async XLA Ops:
  0.0 1.1 copy-start
  1.1 2.4 %copy-start.2 = (bf16[192,2048]{1,0:T(8,128)(2,1)S(1)}, bf16[192,2048]{1,0:T(8,128)(2,1)}, u32[]{:S(2)}) copy-start(bf16[192,2048]{1,0:T(8,128)(2,1)} %x_ref.1) | copy-start | bytes 2359300
  1.1 2.4 %copy-start.3 = (bf16[192,1024]{1,0:T(8,128)(2,1)S(1)}, bf16[192,1024]{1,0:T(8,128)(2,1)}, u32[]{:S(2)}) copy-start(bf16[192,1024]{1,0:T(8,128)(2,1)} %q_ref.1) | copy-start | bytes 1179652
  1.2 2.4 %copy-start.4 = (bf16[192,1024]{1,0:T(8,128)(2,1)S(1)}, bf16[192,1024]{1,0:T(8,128)(2,1)}, u32[]{:S(2)}) copy-start(bf16[192,1024]{1,0:T(8,128)(2,1)} %k_ref.1) | copy-start | bytes 1179652
  1.2 2.4 %copy-start.5 = (bf16[192,1024]{1,0:T(8,128)(2,1)S(1)}, bf16[192,1024]{1,0:T(8,128)(2,1)}, u32[]{:S(2)}) copy-start(bf16[192,1024]{1,0:T(8,128)(2,1)} %v_ref.1) | copy-start | bytes 1179652
  1.2 2.3 %copy-start.6 = (f32[2048]{0:T(1024)S(1)}, f32[2048]{0:T(1024)}, u32[]{:S(2)}) copy-start(f32[2048]{0:T(1024)} %param.15) | copy-start | bytes 24580
  112.2 3.2 %copy-start.1 = (bf16[32,64,2048]{2,1,0:T(8,128)(2,1)}, bf16[32,64,2048]{2,1,0:T(8,128)(2,1)S(1)}, u32[]{:S(2)}) copy-start(bf16[32,64,2048]{2,1,0:T(8,128)(2,1)S(1)} %get-tuple-element.16) | copy-start | bytes 25165828

commit v3 on v2

--- a/solution.py
+++ b/solution.py
@@ -28,6 +28,14 @@
 
 def any_spec():
     return pl.BlockSpec(memory_space=pl.ANY)
+
+
+def hbm_spec():
+    return pl.BlockSpec(memory_space=pltpu.HBM)
+
+
+def in_hbm(a):
+    return pltpu.with_memory_space_constraint(a, pltpu.HBM)
 
 
 def place():
@@ -236,6 +244,7 @@
 
 HALO_COPIES = 8
 W_FIRSTS = (1,)
+HEAD_FIRSTS = (1,)
 
 
 def halo_copies(sends, k_ref, v_ref, kp_ref, vp_ref, relay_ref):
@@ -313,28 +322,56 @@
 
 
 def fine_kernel(
-    x_ref, q_ref, k_ref, v_ref, w_src, gain_ref,
-    state_ref, pooled_ref, normed_ref,
-    mix_ref, edge_out, edge_in, kp_ref, vp_ref, relay_ref, w_ref, local_sem, send_sem, recv_sem,
+    gain_ref, x_src, q_src, k_src, v_src, w_src, wq_ref, wk_ref, wv_ref,
+    state_ref, pooled_ref, normed_ref, head_ref,
+    x_ref, q_ref, k_ref, v_ref,
+    mix_ref, edge_out, edge_in, kp_ref, vp_ref, relay_ref, w_ref, piece_ref,
+    load_sem, local_sem, scatter_send, scatter_recv, send_sem, recv_sem,
 ):
     rows = q_ref.shape[0]
     heads = q_ref.shape[1] // HE
-    position = lax.axis_index("outer") * 16 + lax.axis_index("inner")
+    outer = lax.axis_index("outer")
+    inner = lax.axis_index("inner")
+    position = outer * 16 + inner
     greet(
         plane_neighbours()
         + [device_of(position + d) for d in (2, -2, 1, -1)]
         + [relay_target()]
+        + [(outer, (inner + d) % 16) for d in range(1, 16)]
     )
     sends = Sends(send_sem, recv_sem, HALO_COPIES)
-    weights = plane_gather(sends, w_src, w_ref, local_sem, W_FIRSTS)
-    rows_before = halo_copies(sends, k_ref, v_ref, kp_ref, vp_ref, relay_ref)
+    weights = plane_gather(sends, half_rows(w_src), w_ref, local_sem.at[0], W_FIRSTS)
+    head = plane_gather(sends, piece_ref, head_ref, local_sem.at[1], HEAD_FIRSTS)
+    pieces = scatter((wq_ref, wk_ref, wv_ref), piece_ref, local_sem.at[pl.ds(2, 3)], scatter_send, scatter_recv)
+    rows_before = halo_copies(sends, k_src, v_src, kp_ref, vp_ref, relay_ref)
+    next(weights)
+    next(rows_before)
+    next(pieces)
+    loads = [
+        pltpu.make_async_copy(src, dst, load_sem.at[n])
+        for n, (src, dst) in enumerate(
+            ((q_src, q_ref), (k_src, k_ref), (v_src, v_ref), (x_src, x_ref))
+        )
+    ]
+    for load in loads:
+        load.start()
     next(weights)
     next(rows_before)
     next(weights)
     next(rows_before)
     next(weights)
+    next(rows_before)
+    next(pieces)
+    next(head)
+    next(weights)
+    next(rows_before)
+    next(head)
+    next(weights)
+    next(rows_before)
+    next(head)
     run_all(rows_before)
-    next(weights)
+    for load in loads:
+        load.wait()
     t_prev = lax.broadcasted_iota(jnp.int32, (rows, WIN), 0)
     u_prev = lax.broadcasted_iota(jnp.int32, (rows, WIN), 1)
     ok_prev = (u_prev > t_prev) & (position * rows - WIN + u_prev >= 0)
@@ -357,18 +394,21 @@
         mixed = jnp.dot(p_prev.astype(BF), vp_ref[:, cols], preferred_element_type=F32)
         mixed += jnp.dot(p_own.astype(BF), v_ref[:, cols], preferred_element_type=F32)
         mix_ref[:, cols] = (mixed / total).astype(BF)
-        if h in (1, 3):
-            next(weights)
+        if h in (1, 3, 5):
+            next(head)
     run_all(weights)
     width = x_ref.shape[1]
     half = w_ref.shape[1]
     per = w_ref.shape[2]
 
-    @pl.loop(0, NP // 2)
-    def _(n):
-        at = pl.ds(pl.multiple_of(n * per, per), per)
-        prod = jnp.dot(mix_ref[:, :half], w_ref[n], preferred_element_type=F32)
-        prod += jnp.dot(mix_ref[:, half:], w_ref[n + NP // 2], preferred_element_type=F32)
+    @pl.loop(0, NP // 4)
+    def _(m):
+        n = 2 * m
+        at = pl.ds(pl.multiple_of(n * per, 2 * per), 2 * per)
+        upper = jnp.concatenate([w_ref[n], w_ref[n + 1]], axis=1)
+        lower = jnp.concatenate([w_ref[n + NP // 2], w_ref[n + 1 + NP // 2]], axis=1)
+        prod = jnp.dot(mix_ref[:, :half], upper, preferred_element_type=F32)
+        prod += jnp.dot(mix_ref[:, half:], lower, preferred_element_type=F32)
         state_ref[:, at] = (x_ref[:, at].astype(F32) + prod).astype(BF)
 
     edge_out[...] = state_ref[rows - POOL :, :]
@@ -393,169 +433,197 @@
     wide = pooled.astype(F32)
     moment = jnp.mean(wide * wide, axis=-1, keepdims=True)
     normed_ref[...] = (wide * lax.rsqrt(moment + 1e-06) * gain_ref[...]).astype(BF)
+    run_all(head)
     sends.drain()
 
 
-EDGE_COPY = HALO_COPIES + plane_copies(W_FIRSTS)
-
-
-def fine_stage(x, q, k, v, w_half, gain):
+EDGE_COPY = HALO_COPIES + plane_copies(W_FIRSTS) + plane_copies(HEAD_FIRSTS)
+
+
+def fine_stage(x, q, k, v, gain, w, *head_weights):
     rows, width = x.shape
     coarse = jax.ShapeDtypeStruct((rows // POOL, width), BF)
+    piece = (width // NP, len(head_weights) * HE)
     return pl.pallas_call(
         fine_kernel,
-        out_shape=[jax.ShapeDtypeStruct((rows, width), BF), coarse, coarse],
-        in_specs=[vmem_spec()] * 6,
-        out_specs=[vmem_spec()] * 3,
+        out_shape=[
+            jax.ShapeDtypeStruct((rows, width), BF),
+            coarse,
+            coarse,
+            jax.ShapeDtypeStruct((NP, *piece), BF),
+        ],
+        in_specs=[vmem_spec()] + [hbm_spec()] * 8,
+        out_specs=[vmem_spec()] * 3 + [any_spec()],
         scratch_shapes=[
+            *[pltpu.VMEM(a.shape, BF) for a in (x, q, k, v)],
             pltpu.VMEM(q.shape, BF),
             pltpu.VMEM((POOL, width), BF),
             pltpu.VMEM((POOL, width), BF),
             pltpu.VMEM((WIN, k.shape[1]), BF),
             pltpu.VMEM((WIN, k.shape[1]), BF),
             pltpu.VMEM((2, WIN - 2 * rows, k.shape[1]), BF),
-            pltpu.VMEM((NP, *w_half.shape), BF),
-            pltpu.SemaphoreType.DMA,
+            pltpu.VMEM((NP, w.shape[0] // 2, w.shape[1]), BF),
+            pltpu.VMEM(piece, BF),
+            pltpu.SemaphoreType.DMA((4,)),
+            pltpu.SemaphoreType.DMA((5,)),
+            pltpu.SemaphoreType.DMA((3, 15)),
+            pltpu.SemaphoreType.DMA((3,)),
             pltpu.SemaphoreType.DMA((EDGE_COPY + 1,)),
             pltpu.SemaphoreType.DMA((EDGE_COPY + 1,)),
         ],
         compiler_params=pltpu.CompilerParams(
-            collective_id=2, has_side_effects=True, vmem_limit_bytes=40 << 20
+            collective_id=2, has_side_effects=True, vmem_limit_bytes=32 << 20
         ),
         name="fine",
-    )(x, q, k, v, w_half, gain.reshape(1, width))
+    )(gain.reshape(1, width), *[in_hbm(a) for a in (x, q, k, v, w, *head_weights)])
 
 
 ZCHUNK = 8
-HEAD_FIRSTS = (0, 1)
 
 
 def z_copies(rows):
     return (NZ - 1) * (rows // ZCHUNK)
 
 
+LEAP = 4
+
+
 def z_gather(sends, src_ref, dst_ref, local_sem):
     x, y, z, c = place()
-    up, down = device_at(x, y, (z + 1) % NZ, c), device_at(x, y, (z + NZ - 1) % NZ, c)
     chunks = src_ref.shape[0] // ZCHUNK
     first = sends.next
     sends.next += z_copies(src_ref.shape[0])
-    count_up, count_down = NZ // 2, NZ // 2 - 1
+    ways = ((1, NZ // 2, first), (-1, NZ // 2 - 1, first + NZ // 2 * chunks))
     local = pltpu.make_async_copy(src_ref, dst_ref.at[z], local_sem)
-    for s in range(count_up + 1):
+
+    def far(d):
+        return device_at(x, y, (z + d + NZ) % NZ, c)
+
+    def reach(d, direct):
+        return LEAP if direct else 1
+
+    def send(d, part, way):
+        sign, count, base = way
+        if d > count:
+            return
+        at = pl.ds(part * ZCHUNK, ZCHUNK)
+        own = d in (1, LEAP)
+        held = z if own else (z - sign * (d - 1) + NZ) % NZ
+        src = src_ref.at[at] if own else dst_ref.at[held, at]
+        sends.start(
+            base + (d - 1) * chunks + part, src, dst_ref.at[held, at], far(sign * reach(d, d == LEAP))
+        )
+
+    def receive(d, part, way):
+        sign, count, base = way
+        if d > count:
+            return
+        at = pl.ds(part * ZCHUNK, ZCHUNK)
+        held = (z - sign * d + NZ) % NZ
+        sends.arrived(
+            base + (d - 1) * chunks + part, dst_ref.at[held, at], far(-sign * reach(d, d == LEAP))
+        )
+
+    for d in (1, LEAP):
         for part in range(chunks):
-            at = pl.ds(part * ZCHUNK, ZCHUNK)
-            for sign, count, base, to, origin in (
-                (-1, count_up, first, up, down),
-                (1, count_down, first + count_up * chunks, down, up),
-            ):
-                if s > count:
-                    continue
-                held = (z + sign * s + NZ) % NZ
-                if s > 0:
-                    sends.arrived(base + (s - 1) * chunks + part, dst_ref.at[held, at], origin)
-                if s < count:
-                    src = src_ref.at[at] if s == 0 else dst_ref.at[held, at]
-                    sends.start(base + s * chunks + part, src, dst_ref.at[held, at], to)
-        if s == 0:
-            local.start()
-        if s == count_up:
+            for way in ways:
+                send(d, part, way)
+    local.start()
+    yield
+    for d in (1, 4, 2, 5, 3, 6, 7, 8):
+        for part in range(chunks):
+            for way in ways:
+                receive(d, part, way)
+                if d + 1 not in (LEAP, NZ // 2 + 1):
+                    send(d + 1, part, way)
+        if d == NZ // 2:
             local.wait()
         yield
 
 
-def scatter(src_ref, dst_ref, local_sem, send_sem, recv_sem):
+def scatter(weights, dst_ref, local_sem, send_sem, recv_sem):
     outer = lax.axis_index("outer")
     inner = lax.axis_index("inner")
     head = outer // 2
+    rows = dst_ref.shape[0]
+    base = (outer % 2) * (16 * rows)
+    columns = [pl.ds(n * HE, HE) for n in range(len(weights))]
+
+    def rows_of(w, to):
+        return w.at[pl.ds(pl.multiple_of(base + to * rows, rows), rows)]
+
+    def to_self(n, w):
+        return pltpu.make_async_copy(rows_of(w, inner), dst_ref.at[:, columns[n]], local_sem.at[n])
 
     @pl.when(inner == head)
     def _():
-        pltpu.make_async_copy(src_ref.at[inner], dst_ref, local_sem).start()
+        for n, w in enumerate(weights):
+            to_self(n, w).start()
         for d in range(1, 16):
             to = (inner + d) % 16
-            pltpu.make_async_remote_copy(
-                src_ref=src_ref.at[to],
-                dst_ref=dst_ref,
-                send_sem=send_sem.at[d - 1],
-                recv_sem=recv_sem,
-                device_id=(outer, to),
-                device_id_type=MESH,
-            ).start()
+            for n, w in enumerate(weights):
+                pltpu.make_async_remote_copy(
+                    src_ref=rows_of(w, to),
+                    dst_ref=dst_ref.at[:, columns[n]],
+                    send_sem=send_sem.at[n, d - 1],
+                    recv_sem=recv_sem.at[n],
+                    device_id=(outer, to),
+                    device_id_type=MESH,
+                ).start()
 
     yield
 
     @pl.when(inner == head)
     def _():
-        pltpu.make_async_copy(src_ref.at[inner], dst_ref, local_sem).wait()
-        for d in range(1, 16):
-            pltpu.make_async_copy(src_ref.at[0], src_ref.at[0], send_sem.at[d - 1]).wait()
+        for n, w in enumerate(weights):
+            to_self(n, w).wait()
+            for d in range(1, 16):
+                piece = rows_of(w, 0)
+                pltpu.make_async_copy(piece, piece, send_sem.at[n, d - 1]).wait()
 
     @pl.when(inner != head)
     def _():
-        pltpu.make_async_copy(dst_ref, dst_ref, recv_sem).wait()
-
-    yield
+        for n in range(len(weights)):
+            piece = dst_ref.at[:, columns[n]]
+            pltpu.make_async_copy(piece, piece, recv_sem.at[n]).wait()
+
+    yield
+
+
+def half_rows(w_ref):
+    size = w_ref.shape[0] // 2
+    copy = lax.axis_index("outer") % 2
+    return w_ref.at[pl.ds(pl.multiple_of(copy * size, size), size)]
 
 
 def middle_kernel(
-    normed_ref, pieces_ref, w_src, tokens_ref, head_ref, w_ref,
-    piece_ref, local_sem, scatter_send, scatter_recv, send_sem, recv_sem,
+    normed_ref, w_src, tokens_ref, w_ref, local_sem, send_sem, recv_sem
 ):
     x, y, z, c = place()
-    outer = lax.axis_index("outer")
-    inner = lax.axis_index("inner")
-    ends = [device_at(x, y, (z + 1) % NZ, c), device_at(x, y, (z + NZ - 1) % NZ, c)]
-    greet(plane_neighbours() + ends + [(outer, (inner + d) % 16) for d in range(1, 16)])
+    greet(plane_neighbours() + [device_at(x, y, (z + d + NZ) % NZ, c) for d in (1, -1, LEAP, -LEAP)])
     sends = Sends(send_sem, recv_sem)
     along = z_gather(sends, normed_ref, tokens_ref, local_sem.at[0])
-    pieces = scatter(pieces_ref, piece_ref, local_sem.at[1], scatter_send, scatter_recv)
-    head = plane_gather(sends, piece_ref, head_ref, local_sem.at[2], HEAD_FIRSTS)
-    out = plane_gather(sends, w_src, w_ref, local_sem.at[3])
-    next(along)
-    next(pieces)
-    next(out)
-    next(along)
-    next(along)
-    next(pieces)
-    next(head)
-    next(out)
-    next(along)
-    next(head)
-    next(out)
-    next(along)
-    next(head)
-    next(out)
-    next(along)
-    next(head)
-    next(out)
-    next(along)
-    next(head)
-    next(out)
-    next(along)
-    next(head)
-    next(along)
-    run_all(head)
+    out = plane_gather(sends, half_rows(w_src), w_ref, local_sem.at[1])
+    for steps in (1, 2, 2, 1, 2, 1):
+        for _ in range(steps):
+            next(along)
+        next(out)
     run_all(out)
     sends.drain()
 
 
-def middle_stage(normed, pieces, w_half):
-    count = z_copies(normed.shape[0]) + plane_copies(HEAD_FIRSTS) + plane_copies((0, 1))
+def middle_stage(normed, w):
+    count = z_copies(normed.shape[0]) + plane_copies((0, 1))
     return pl.pallas_call(
         middle_kernel,
         out_shape=[
             jax.ShapeDtypeStruct((NZ, *normed.shape), BF),
-            jax.ShapeDtypeStruct((NP, *pieces.shape[1:]), BF),
-            jax.ShapeDtypeStruct((NP, *w_half.shape), BF),
+            jax.ShapeDtypeStruct((NP, w.shape[0] // 2, w.shape[1]), BF),
         ],
-        in_specs=[any_spec()] * 3,
-        out_specs=[any_spec()] * 3,
+        in_specs=[any_spec(), hbm_spec()],
+        out_specs=[any_spec(), hbm_spec()],
         scratch_shapes=[
-            pltpu.VMEM(pieces.shape[1:], BF),
-            pltpu.SemaphoreType.DMA((4,)),
-            pltpu.SemaphoreType.DMA((15,)),
-            pltpu.SemaphoreType.DMA,
+            pltpu.SemaphoreType.DMA((2,)),
             pltpu.SemaphoreType.DMA((count,)),
             pltpu.SemaphoreType.DMA((count,)),
         ],
@@ -563,7 +631,7 @@
             collective_id=3, has_side_effects=True, vmem_limit_bytes=16 << 20
         ),
         name="middle",
-    )(normed, pieces, w_half)
+    )(normed, w)
 
 
 KEY_GROUP = 8
@@ -571,14 +639,14 @@
 
 
 def coarse_kernel(
-    proj_ref, out_ref,
-    kv_ref, top_ref, acc_ref, mix_ref, heads_ref, local_sem, send_sem, recv_sem,
+    proj_ref, pooled_ref, w_src, out_ref,
+    kv_ref, top_ref, acc_ref, mix_ref, heads_ref, w_ref, local_sem, w_sem, send_sem, recv_sem,
 ):
     x, y, z, c = place()
     others = [device_at(x, y, (z + d) % NZ, c) for d in range(1, NZ)]
     greet(plane_neighbours() + others)
     sends = Sends(send_sem, recv_sem, NZ - 1)
-    run_all(plane_gather(sends, proj_ref.at[:, HE:], kv_ref, local_sem))
+    gather = plane_gather(sends, proj_ref.at[:, HE:], kv_ref, local_sem)
     me = slot_of(x, y, c)
     count = proj_ref.shape[0]
     per = count // NZ
@@ -591,16 +659,17 @@
     t = lax.broadcasted_iota(jnp.int32, (step, 1), 0)
     u = lax.broadcasted_iota(jnp.int32, (1, width), 1)
     t_order = (t // per * NP + me) * 32 + t % per
-    u_order = (u % step // per * NP + u // step) * 32 + u % per
-
-    @pl.loop(0, NP // KEY_GROUP)
-    def _(g):
-        some = pl.ds(g * KEY_GROUP, KEY_GROUP)
-        allowed = u_order <= t_order - g * (KEY_GROUP * 32)
+    u_order = u % step // per * (NP * 32) + u % per
+
+    def attend(slots):
+        order = u_order
+        for i, slot in enumerate(slots):
+            order = jnp.where(u // step == i, order + slot * 32, order)
+        allowed = order <= t_order
         for n in range(NZ // PLANE_GROUP):
             lo = n * step
-            keys = kv_ref[some, lo : lo + step, :HE].reshape(width, HE)
-            values = kv_ref[some, lo : lo + step, HE:].reshape(width, HE)
+            keys = jnp.concatenate([kv_ref[d, lo : lo + step, :HE] for d in slots], axis=0)
+            values = jnp.concatenate([kv_ref[d, lo : lo + step, HE:] for d in slots], axis=0)
             s = lax.dot_general(
                 proj_ref[lo:, :HE], keys, TRANS, preferred_element_type=F32
             ) * factor
@@ -615,6 +684,26 @@
             )
             top_ref[lo:, :] = new
 
+    def slots_at(offsets, core):
+        return [slot_of((x + a) % NX, (y + b) % NY, core) for a, b in offsets]
+
+    early = [(0, 1), (0, 3), (1, 0), (3, 0), (1, 1), (1, 3), (3, 1), (3, 3)]
+    late = [(0, 0), (0, 2), (2, 0), (2, 1), (2, 3), (1, 2), (3, 2), (2, 2)]
+    next(gather)
+    inners = w_ref.shape[0]
+    loads = [
+        pltpu.make_async_copy(w_src.at[pl.ds(n * inners, inners)], w_ref.at[:, n], w_sem.at[n])
+        for n in range(w_ref.shape[1])
+    ]
+    for load in loads:
+        load.start()
+    for _ in range(5):
+        next(gather)
+    attend(slots_at(early, c))
+    run_all(gather)
+    attend(slots_at(late, c))
+    attend(slots_at(early, 1 - c))
+    attend(slots_at(late, 1 - c))
     mix_ref[...] = (acc_ref[:, :HE] / acc_ref[:, HE:]).astype(BF).reshape(mix_ref.shape)
     for d in (8, 7, 9, 6, 10, 5, 11, 4, 12, 3, 13, 2, 14, 1, 15):
         sends.start(d - 1, mix_ref.at[(z + d) % NZ], heads_ref.at[z], others[d - 1])
@@ -623,16 +712,24 @@
         origin = (z + NZ - d) % NZ
         sends.arrived(d - 1, heads_ref.at[origin], others[NZ - d - 1])
     sends.drain()
-    out_ref[...] = heads_ref[...]
-
-
-def coarse_stage(proj):
+    for load in loads:
+        load.wait()
+    total = pooled_ref[...].astype(F32)
+    depth = 2 * HE
+    for n in range(NZ // 2):
+        two = jnp.concatenate([heads_ref[2 * n], heads_ref[2 * n + 1]], axis=1)
+        w = w_ref[2 * n : 2 * n + 2].reshape(depth, total.shape[1])
+        total += jnp.dot(two, w, preferred_element_type=F32)
+    out_ref[...] = total.astype(BF)
+
+
+def coarse_stage(proj, pooled, w):
     rows = proj.shape[0]
     count = NZ - 1 + plane_copies((0, 1))
     return pl.pallas_call(
         coarse_kernel,
-        out_shape=jax.ShapeDtypeStruct((NZ, rows // NZ, HE), BF),
-        in_specs=[vmem_spec()],
+        out_shape=jax.ShapeDtypeStruct(pooled.shape, BF),
+        in_specs=[vmem_spec(), vmem_spec(), hbm_spec()],
         out_specs=vmem_spec(),
         scratch_shapes=[
             pltpu.VMEM((NP, rows, 2 * HE), BF),
@@ -640,15 +737,17 @@
             pltpu.VMEM((rows, 2 * HE), F32),
             pltpu.VMEM((NZ, rows // NZ, HE), BF),
             pltpu.VMEM((NZ, rows // NZ, HE), BF),
+            pltpu.VMEM((NP // 2, 2, *w.shape[1:]), BF),
             pltpu.SemaphoreType.DMA,
+            pltpu.SemaphoreType.DMA((2,)),
             pltpu.SemaphoreType.DMA((count,)),
             pltpu.SemaphoreType.DMA((count,)),
         ],
         compiler_params=pltpu.CompilerParams(
-            collective_id=4, has_side_effects=True, vmem_limit_bytes=40 << 20
+            collective_id=4, has_side_effects=True, vmem_limit_bytes=36 << 20
         ),
         name="coarse",
-    )(proj)
+    )(proj, pooled, w)
 
 
 def on_device(
@@ -664,27 +763,14 @@
     w_coarse_out,
 ):
     rows, width = fine_input.shape
-    copy = lax.axis_index("outer") % 2
-
-    def half_of(w):
-        size = w.shape[0] // 2
-        return lax.dynamic_slice_in_dim(w, copy * size, size, 0)
-
-    state, pooled, normed = fine_stage(
-        fine_input, fine_query, fine_key, fine_value, half_of(w_fine_out), norm_gain
+    state, pooled, normed, w_head = fine_stage(
+        fine_input, fine_query, fine_key, fine_value, norm_gain, w_fine_out, w_query, w_key, w_value
     )
-    joined = jnp.concatenate([half_of(w_query), half_of(w_key), half_of(w_value)], axis=1)
-    pieces = joined.reshape(16, -1, joined.shape[1])
-    tokens, w_head, w_out = middle_stage(normed, pieces, half_of(w_coarse_out))
+    tokens, w_out = middle_stage(normed, w_coarse_out)
     proj = jnp.dot(
         tokens.reshape(-1, width), w_head.reshape(width, -1), preferred_element_type=F32
     ).astype(BF)
-    heads = coarse_stage(proj)
-    heads = heads.reshape(NZ, rows // POOL, 2, HE // 2).transpose(1, 2, 0, 3)
-    head_total = jnp.dot(
-        heads.reshape(rows // POOL, -1), w_out.reshape(-1, width), preferred_element_type=F32
-    )
-    coarse_out = (pooled.astype(F32) + head_total).astype(BF)
+    coarse_out = coarse_stage(proj, pooled, w_out)
     groups = state.reshape(rows // POOL, POOL, width).astype(F32)
     lifted = groups + coarse_out.astype(F32)[:, None, :]
     return lifted.reshape(rows, width).astype(BF)

time: 167 us -> 159 us (0.952)
  local copies, waits for them, and re-layouts: 6.94 us -> 0.7 us
  matrix products: 5.55 us -> 0.98 us
  Pallas kernels: 153 us -> 156 us
    pallas_call x1, Pallas kernels: 58.2 us -> 71.1 us  [fine_stage(): pl.pallas_call(fine_kernel, out_shape=[jax.ShapeDtypeStruct((rows, width)...]
    pallas_call x1, Pallas kernels: 50.5 us -> 41.4 us  [middle_stage(): pl.pallas_call(middle_kernel, out_shape=[jax.ShapeDtypeStruct((NZ, *norme...]
    dot_general x1 -> x0, matrix products: 4.58 us -> none  [on_device(): jnp.dot(heads.reshape(rows // POOL, -1), w_out.reshape(-1, width), prefer...]
    dynamic_slice x4 -> x0, local copies, waits for them, and re-layouts: 3.17 us -> none  [half_of(): return lax.dynamic_slice_in_dim(w, copy * size, size, 0)]
    unnamed x14 -> x4, local copies, waits for them, and re-layouts: 3.38 us -> 0.7 us
where the time goes in v3:
time: 159 us
  Pallas kernels  156 us (98%)
    pallas_call x1, Pallas kernels, fine_stage(): pl.pallas_call(fine_kernel, out_shape=[jax.ShapeDtypeStruct((rows, width)...  71.1 us
    pallas_call x1, Pallas kernels, coarse_stage(): pl.pallas_call(coarse_kernel, out_shape=jax.ShapeDtypeStruct(pooled.shape...  43.4 us
    pallas_call x1, Pallas kernels, middle_stage(): pl.pallas_call(middle_kernel, out_shape=[jax.ShapeDtypeStruct((NZ, *norme...  41.4 us

profile of v3, /device:TPU:1, one launch (start us, length us, event | category | flops | bytes accessed | tf_op | source)
XLA Modules:
  0.0 158.7 jit_solution(2308708778167577741)
XLA Ops:
  0.0 0.0 copy-start.1
  0.0 0.7 copy-done.1
  0.7 0.0 copy-start
  0.7 71.1 %fine.1 = (bf16[192,2048]{1,0:T(8,128)(2,1)S(1)}, bf16[24,2048]{1,0:T(8,128)(2,1)S(1)}, bf16[24,2048]{1,0:T(8,128)(2,1)S(1)}, bf16[32,64,384]{2,1,0:T(8,128)(2,1)S(1)}) custom-call(f32[1,2048]{1,0:T(1,128)S(1)} %bitcast.9, bf16[192,2048]{1,0:T(8,128)(2,1)} %x_src.1, bf16[192,1024]{1,0:T(8,128)(2,1)} %q_src.1, bf16[192,1024]{1,0:T(8,128)(2,1)} %k_src.1, ...), custom_call_target="tpu_custom_call" | custom-call | tf_op jit(solution)/shard_map/fine/pallas_call | solution.py:447
  71.8 0.0 copy-done
  71.8 41.4 %middle.1 = (bf16[16,24,2048]{2,1,0:T(8,128)(2,1)S(1)}, bf16[32,64,2048]{2,1,0:T(8,128)(2,1)S(1)}) custom-call(bf16[24,2048]{1,0:T(8,128)(2,1)S(1)} %get-tuple-element.12.normed_ref, bf16[128,2048]{1,0:T(8,128)(2,1)S(1)} %copy-done), custom_call_target="tpu_custom_call" | custom-call | tf_op jit(solution)/shard_map/middle/pallas_call | solution.py:617
  113.2 1.0 convolution_convert_fusion.proj_ref
  114.2 43.4 %coarse.1 = bf16[24,2048]{1,0:T(8,128)(2,1)S(1)} custom-call(bf16[384,384]{1,0:T(8,128)(2,1)S(1)} %convolution_convert_fusion.proj_ref, bf16[24,2048]{1,0:T(8,128)(2,1)S(1)} %get-tuple-element.15.pooled_ref, bf16[32,64,2048]{2,1,0:T(8,128)(2,1)S(1)} %get-tuple-element.16.w_src), custom_call_target="tpu_custom_call" | custom-call | tf_op jit(solution)/shard_map/coarse/pallas_call | solution.py:729
  157.7 1.1 fusion
  (1 shorter events, 0.0 us)
Async XLA Ops:
  0.0 0.7 copy-start.1
  0.7 71.1 %copy-start = (bf16[128,2048]{1,0:T(8,128)(2,1)S(1)}, bf16[128,2048]{1,0:T(8,128)(2,1)}, u32[]{:S(2)}) copy-start(bf16[128,2048]{1,0:T(8,128)(2,1)} %w_src.3) | copy-start | bytes 1572868

commit v4 on v3

--- a/solution.py
+++ b/solution.py
@@ -242,9 +242,9 @@
         pass
 
 
-HALO_COPIES = 8
+HALO_PARTS = 4
+HALO_COPIES = 4 * HALO_PARTS
 W_FIRSTS = (1,)
-HEAD_FIRSTS = (1,)
 
 
 def halo_copies(sends, k_ref, v_ref, kp_ref, vp_ref, relay_ref):
@@ -256,7 +256,13 @@
     partner = device_at(x, y, z, 1 - c)
     down, up = device_at(x, (y + 3) % NY, z, c), device_at(x, (y + 1) % NY, z, c)
     relay_to = relay_target()
-    pairs = ((k_ref, kp_ref), (v_ref, vp_ref))
+    half = k_ref.shape[1] // 2
+    pairs = [
+        (own.at[:, pl.ds(lo, half)], prev.at[:, pl.ds(lo, half)])
+        for lo in (0, half)
+        for own, prev in ((k_ref, kp_ref), (v_ref, vp_ref))
+    ]
+    count = len(pairs)
     mid, end = pl.ds(short, rows), pl.ds(short + rows, rows)
     head, tail = pl.ds(0, short), pl.ds(rows - short, short)
 
@@ -268,11 +274,11 @@
 
         @pl.when(c == 0)
         def _():
-            put(2 + n, own, prev.at[end], partner)
+            put(count + n, own, prev.at[end], partner)
 
         @pl.when(c == 1)
         def _():
-            put(6 + n, own.at[tail], relay_ref.at[n], down)
+            put(3 * count + n, own.at[tail], relay_ref.at[n], down)
 
         yield
 
@@ -280,34 +286,37 @@
 
         @pl.when(c == 1)
         def _():
-            sends.copy(6 + n, relay_ref.at[n], relay_ref.at[n], up).wait_recv()
-            put(4 + n, relay_ref.at[n], prev.at[head], relay_to)
+            sends.copy(3 * count + n, relay_ref.at[n], relay_ref.at[n], up).wait_recv()
+            put(2 * count + n, relay_ref.at[n], prev.at[head], relay_to)
 
         yield
-    for n, (own, prev) in enumerate(pairs):
-        sends.arrived(n, prev.at[mid], behind)
-
-        @pl.when(c == 0)
-        def _():
-            put(4 + n, prev.at[pl.ds(rows, short)], prev.at[head], partner)
-
-        @pl.when(c == 1)
-        def _():
-            put(2 + n, prev.at[mid], prev.at[end], partner)
-
-        yield
-    for n, (own, prev) in enumerate(pairs):
-        sends.arrived(2 + n, prev.at[end], partner)
-        sends.arrived(4 + n, prev.at[head], partner)
-        sends.copy(n, own, prev.at[mid], ahead).wait_send()
-        sends.copy(2 + n, own, prev.at[end], partner).wait_send()
-        sends.copy(4 + n, own.at[tail], prev.at[head], partner).wait_send()
-
-        @pl.when(c == 1)
-        def _():
-            sends.copy(6 + n, own.at[tail], relay_ref.at[n], down).wait_send()
-
-    yield
+    for group in (range(count // 2), range(count // 2, count)):
+        for n in group:
+            own, prev = pairs[n]
+            sends.arrived(n, prev.at[mid], behind)
+
+            @pl.when(c == 0)
+            def _():
+                put(2 * count + n, prev.at[pl.ds(rows, short)], prev.at[head], partner)
+
+            @pl.when(c == 1)
+            def _():
+                put(count + n, prev.at[mid], prev.at[end], partner)
+
+            yield
+        for n in group:
+            own, prev = pairs[n]
+            sends.arrived(count + n, prev.at[end], partner)
+            sends.arrived(2 * count + n, prev.at[head], partner)
+            sends.copy(n, own, prev.at[mid], ahead).wait_send()
+            sends.copy(count + n, own, prev.at[end], partner).wait_send()
+            sends.copy(2 * count + n, own.at[tail], prev.at[head], partner).wait_send()
+
+            @pl.when(c == 1)
+            def _():
+                sends.copy(3 * count + n, own.at[tail], relay_ref.at[n], down).wait_send()
+
+            yield
 
 
 def relay_target():
@@ -322,56 +331,40 @@
 
 
 def fine_kernel(
-    gain_ref, x_src, q_src, k_src, v_src, w_src, wq_ref, wk_ref, wv_ref,
-    state_ref, pooled_ref, normed_ref, head_ref,
-    x_ref, q_ref, k_ref, v_ref,
-    mix_ref, edge_out, edge_in, kp_ref, vp_ref, relay_ref, w_ref, piece_ref,
-    load_sem, local_sem, scatter_send, scatter_recv, send_sem, recv_sem,
+    gain_ref, x_src, q_src, k_src, v_src, w_src,
+    state_ref, pooled_ref, normed_ref,
+    x_ref, q_ref, k_ref, v_ref, mix_ref, edge_out, edge_in, kp_ref, vp_ref, relay_ref, w_ref,
+    load_sem, local_sem, send_sem, recv_sem,
 ):
     rows = q_ref.shape[0]
     heads = q_ref.shape[1] // HE
-    outer = lax.axis_index("outer")
-    inner = lax.axis_index("inner")
-    position = outer * 16 + inner
+    position = lax.axis_index("outer") * 16 + lax.axis_index("inner")
     greet(
         plane_neighbours()
         + [device_of(position + d) for d in (2, -2, 1, -1)]
         + [relay_target()]
-        + [(outer, (inner + d) % 16) for d in range(1, 16)]
     )
     sends = Sends(send_sem, recv_sem, HALO_COPIES)
-    weights = plane_gather(sends, half_rows(w_src), w_ref, local_sem.at[0], W_FIRSTS)
-    head = plane_gather(sends, piece_ref, head_ref, local_sem.at[1], HEAD_FIRSTS)
-    pieces = scatter((wq_ref, wk_ref, wv_ref), piece_ref, local_sem.at[pl.ds(2, 3)], scatter_send, scatter_recv)
-    rows_before = halo_copies(sends, k_src, v_src, kp_ref, vp_ref, relay_ref)
-    next(weights)
-    next(rows_before)
-    next(pieces)
+    weights = plane_gather(sends, half_rows(w_src), w_ref, local_sem, W_FIRSTS)
+    before_rows = halo_copies(sends, k_src, v_src, kp_ref, vp_ref, relay_ref)
     loads = [
         pltpu.make_async_copy(src, dst, load_sem.at[n])
         for n, (src, dst) in enumerate(
             ((q_src, q_ref), (k_src, k_ref), (v_src, v_ref), (x_src, x_ref))
         )
     ]
+    next(weights)
+    next(before_rows)
+    next(before_rows)
     for load in loads:
         load.start()
-    next(weights)
-    next(rows_before)
-    next(weights)
-    next(rows_before)
-    next(weights)
-    next(rows_before)
-    next(pieces)
-    next(head)
-    next(weights)
-    next(rows_before)
-    next(head)
-    next(weights)
-    next(rows_before)
-    next(head)
-    run_all(rows_before)
+    for steps in (weights, before_rows, before_rows, weights, before_rows, before_rows, weights):
+        next(steps)
+    for steps in (before_rows,) * 4 + (weights,) + (before_rows,) * 2:
+        next(steps)
     for load in loads:
         load.wait()
+    between = {0: (weights,), 1: (before_rows,), 2: (before_rows,), 3: (before_rows,) * 2, 5: (weights,)}
     t_prev = lax.broadcasted_iota(jnp.int32, (rows, WIN), 0)
     u_prev = lax.broadcasted_iota(jnp.int32, (rows, WIN), 1)
     ok_prev = (u_prev > t_prev) & (position * rows - WIN + u_prev >= 0)
@@ -394,9 +387,8 @@
         mixed = jnp.dot(p_prev.astype(BF), vp_ref[:, cols], preferred_element_type=F32)
         mixed += jnp.dot(p_own.astype(BF), v_ref[:, cols], preferred_element_type=F32)
         mix_ref[:, cols] = (mixed / total).astype(BF)
-        if h in (1, 3, 5):
-            next(head)
-    run_all(weights)
+        for steps in between.get(h, ()):
+            next(steps)
     width = x_ref.shape[1]
     half = w_ref.shape[1]
     per = w_ref.shape[2]
@@ -433,27 +425,20 @@
     wide = pooled.astype(F32)
     moment = jnp.mean(wide * wide, axis=-1, keepdims=True)
     normed_ref[...] = (wide * lax.rsqrt(moment + 1e-06) * gain_ref[...]).astype(BF)
-    run_all(head)
     sends.drain()
 
 
-EDGE_COPY = HALO_COPIES + plane_copies(W_FIRSTS) + plane_copies(HEAD_FIRSTS)
-
-
-def fine_stage(x, q, k, v, gain, w, *head_weights):
+EDGE_COPY = HALO_COPIES + plane_copies(W_FIRSTS)
+
+
+def fine_stage(x, q, k, v, gain, w):
     rows, width = x.shape
     coarse = jax.ShapeDtypeStruct((rows // POOL, width), BF)
-    piece = (width // NP, len(head_weights) * HE)
     return pl.pallas_call(
         fine_kernel,
-        out_shape=[
-            jax.ShapeDtypeStruct((rows, width), BF),
-            coarse,
-            coarse,
-            jax.ShapeDtypeStruct((NP, *piece), BF),
-        ],
-        in_specs=[vmem_spec()] + [hbm_spec()] * 8,
-        out_specs=[vmem_spec()] * 3 + [any_spec()],
+        out_shape=[jax.ShapeDtypeStruct((rows, width), BF), coarse, coarse],
+        in_specs=[vmem_spec()] + [hbm_spec()] * 5,
+        out_specs=[vmem_spec()] * 3,
         scratch_shapes=[
             *[pltpu.VMEM(a.shape, BF) for a in (x, q, k, v)],
             pltpu.VMEM(q.shape, BF),
@@ -461,13 +446,10 @@
             pltpu.VMEM((POOL, width), BF),
             pltpu.VMEM((WIN, k.shape[1]), BF),
             pltpu.VMEM((WIN, k.shape[1]), BF),
-            pltpu.VMEM((2, WIN - 2 * rows, k.shape[1]), BF),
+            pltpu.VMEM((HALO_PARTS, WIN - 2 * rows, k.shape[1] // 2), BF),
             pltpu.VMEM((NP, w.shape[0] // 2, w.shape[1]), BF),
-            pltpu.VMEM(piece, BF),
             pltpu.SemaphoreType.DMA((4,)),
-            pltpu.SemaphoreType.DMA((5,)),
-            pltpu.SemaphoreType.DMA((3, 15)),
-            pltpu.SemaphoreType.DMA((3,)),
+            pltpu.SemaphoreType.DMA,
             pltpu.SemaphoreType.DMA((EDGE_COPY + 1,)),
             pltpu.SemaphoreType.DMA((EDGE_COPY + 1,)),
         ],
@@ -475,7 +457,7 @@
             collective_id=2, has_side_effects=True, vmem_limit_bytes=32 << 20
         ),
         name="fine",
-    )(gain.reshape(1, width), *[in_hbm(a) for a in (x, q, k, v, w, *head_weights)])
+    )(gain.reshape(1, width), *[in_hbm(a) for a in (x, q, k, v, w)])
 
 
 ZCHUNK = 8
@@ -485,58 +467,32 @@
     return (NZ - 1) * (rows // ZCHUNK)
 
 
-LEAP = 4
-
-
 def z_gather(sends, src_ref, dst_ref, local_sem):
     x, y, z, c = place()
+    up, down = device_at(x, y, (z + 1) % NZ, c), device_at(x, y, (z + NZ - 1) % NZ, c)
     chunks = src_ref.shape[0] // ZCHUNK
     first = sends.next
     sends.next += z_copies(src_ref.shape[0])
-    ways = ((1, NZ // 2, first), (-1, NZ // 2 - 1, first + NZ // 2 * chunks))
+    count_up, count_down = NZ // 2, NZ // 2 - 1
     local = pltpu.make_async_copy(src_ref, dst_ref.at[z], local_sem)
-
-    def far(d):
-        return device_at(x, y, (z + d + NZ) % NZ, c)
-
-    def reach(d, direct):
-        return LEAP if direct else 1
-
-    def send(d, part, way):
-        sign, count, base = way
-        if d > count:
-            return
-        at = pl.ds(part * ZCHUNK, ZCHUNK)
-        own = d in (1, LEAP)
-        held = z if own else (z - sign * (d - 1) + NZ) % NZ
-        src = src_ref.at[at] if own else dst_ref.at[held, at]
-        sends.start(
-            base + (d - 1) * chunks + part, src, dst_ref.at[held, at], far(sign * reach(d, d == LEAP))
-        )
-
-    def receive(d, part, way):
-        sign, count, base = way
-        if d > count:
-            return
-        at = pl.ds(part * ZCHUNK, ZCHUNK)
-        held = (z - sign * d + NZ) % NZ
-        sends.arrived(
-            base + (d - 1) * chunks + part, dst_ref.at[held, at], far(-sign * reach(d, d == LEAP))
-        )
-
-    for d in (1, LEAP):
+    for s in range(count_up + 1):
         for part in range(chunks):
-            for way in ways:
-                send(d, part, way)
-    local.start()
-    yield
-    for d in (1, 4, 2, 5, 3, 6, 7, 8):
-        for part in range(chunks):
-            for way in ways:
-                receive(d, part, way)
-                if d + 1 not in (LEAP, NZ // 2 + 1):
-                    send(d + 1, part, way)
-        if d == NZ // 2:
+            at = pl.ds(part * ZCHUNK, ZCHUNK)
+            for sign, count, base, to, origin in (
+                (-1, count_up, first, up, down),
+                (1, count_down, first + count_up * chunks, down, up),
+            ):
+                if s > count:
+                    continue
+                held = (z + sign * s + NZ) % NZ
+                if s > 0:
+                    sends.arrived(base + (s - 1) * chunks + part, dst_ref.at[held, at], origin)
+                if s < count:
+                    src = src_ref.at[at] if s == 0 else dst_ref.at[held, at]
+                    sends.start(base + s * chunks + part, src, dst_ref.at[held, at], to)
+        if s == 0:
+            local.start()
+        if s == count_up:
             local.wait()
         yield
 
@@ -596,34 +552,80 @@
     return w_ref.at[pl.ds(pl.multiple_of(copy * size, size), size)]
 
 
+PIECE_COPIES = 32
+
+
+def to_all_of_plane(sends, src, dst, local_sem):
+    x, y, z, c = place()
+    partner = device_at(x, y, z, 1 - c)
+    mine = slot_of(x, y, c)
+    first = sends.next
+    sends.next += PIECE_COPIES
+    offsets = [(a, b) for a in range(NX) for b in range(NY)]
+    local = pltpu.make_async_copy(src, dst.at[mine], local_sem)
+    local.start()
+    for n, (a, b) in enumerate(offsets):
+        to = device_at((x + a) % NX, (y + b) % NY, z, c) if n else partner
+        sends.start(first + n, src, dst.at[mine], to)
+    yield
+    for n, (a, b) in enumerate(offsets):
+        if n:
+            px, py = (x + NX - a) % NX, (y + NY - b) % NY
+            s = slot_of(px, py, c)
+            sends.arrived(first + n, dst.at[s], device_at(px, py, z, c))
+            sends.start(first + len(offsets) + n, dst.at[s], dst.at[s], partner)
+    yield
+    local.wait()
+    sends.arrived(first, dst.at[slot_of(x, y, 1 - c)], partner)
+    for n, (a, b) in enumerate(offsets):
+        if n:
+            s = slot_of((x + NX - a) % NX, (y + NY - b) % NY, 1 - c)
+            sends.arrived(first + len(offsets) + n, dst.at[s], partner)
+    yield
+
+
 def middle_kernel(
-    normed_ref, w_src, tokens_ref, w_ref, local_sem, send_sem, recv_sem
+    normed_ref, w_src, wq_ref, wk_ref, wv_ref, tokens_ref, w_ref, head_ref,
+    piece_ref, local_sem, scatter_send, scatter_recv, send_sem, recv_sem,
 ):
     x, y, z, c = place()
-    greet(plane_neighbours() + [device_at(x, y, (z + d + NZ) % NZ, c) for d in (1, -1, LEAP, -LEAP)])
+    outer = lax.axis_index("outer")
+    inner = lax.axis_index("inner")
+    plane = [(a, b) for a in range(NX) for b in range(NY)][1:]
+    greet(
+        [device_at((x + a) % NX, (y + b) % NY, z, c) for a, b in plane]
+        + [device_at(x, y, z, 1 - c)]
+        + [device_at(x, y, (z + d + NZ) % NZ, c) for d in (1, -1)]
+        + [(outer, (inner + d) % 16) for d in range(1, 16)]
+    )
     sends = Sends(send_sem, recv_sem)
     along = z_gather(sends, normed_ref, tokens_ref, local_sem.at[0])
     out = plane_gather(sends, half_rows(w_src), w_ref, local_sem.at[1])
-    for steps in (1, 2, 2, 1, 2, 1):
-        for _ in range(steps):
-            next(along)
-        next(out)
-    run_all(out)
+    pieces = scatter((wq_ref, wk_ref, wv_ref), piece_ref, local_sem.at[pl.ds(2, 3)], scatter_send, scatter_recv)
+    head = to_all_of_plane(sends, piece_ref, head_ref, local_sem.at[5])
+    order = (along, pieces, out, along, along, pieces, head, out, along, out, along, out, along, out)
+    for steps in order + (along, head, along, out, along, head, out):
+        next(steps)
     sends.drain()
 
 
-def middle_stage(normed, w):
-    count = z_copies(normed.shape[0]) + plane_copies((0, 1))
+def middle_stage(normed, w, *head_weights):
+    count = z_copies(normed.shape[0]) + plane_copies((0, 1)) + PIECE_COPIES
+    piece = (normed.shape[1] // NP, len(head_weights) * HE)
     return pl.pallas_call(
         middle_kernel,
         out_shape=[
             jax.ShapeDtypeStruct((NZ, *normed.shape), BF),
             jax.ShapeDtypeStruct((NP, w.shape[0] // 2, w.shape[1]), BF),
+            jax.ShapeDtypeStruct((NP, *piece), BF),
         ],
-        in_specs=[any_spec(), hbm_spec()],
-        out_specs=[any_spec(), hbm_spec()],
+        in_specs=[any_spec()] + [hbm_spec()] * 4,
+        out_specs=[any_spec(), hbm_spec(), any_spec()],
         scratch_shapes=[
-            pltpu.SemaphoreType.DMA((2,)),
+            pltpu.VMEM(piece, BF),
+            pltpu.SemaphoreType.DMA((6,)),
+            pltpu.SemaphoreType.DMA((3, 15)),
+            pltpu.SemaphoreType.DMA((3,)),
             pltpu.SemaphoreType.DMA((count,)),
             pltpu.SemaphoreType.DMA((count,)),
         ],
@@ -631,65 +633,35 @@
             collective_id=3, has_side_effects=True, vmem_limit_bytes=16 << 20
         ),
         name="middle",
-    )(normed, w)
-
-
-KEY_GROUP = 8
+    )(normed, *[in_hbm(a) for a in (w, *head_weights)])
+
+
 PLANE_GROUP = 4
+STATS = 3
 
 
 def coarse_kernel(
     proj_ref, pooled_ref, w_src, out_ref,
-    kv_ref, top_ref, acc_ref, mix_ref, heads_ref, w_ref, local_sem, w_sem, send_sem, recv_sem,
+    kv_ref, q_ref, top_ref, acc_ref, part_out, part_in, mix_ref, heads_ref, w_ref,
+    w_sem, send_sem, recv_sem,
 ):
     x, y, z, c = place()
     others = [device_at(x, y, (z + d) % NZ, c) for d in range(1, NZ)]
-    greet(plane_neighbours() + others)
-    sends = Sends(send_sem, recv_sem, NZ - 1)
-    gather = plane_gather(sends, proj_ref.at[:, HE:], kv_ref, local_sem)
-    me = slot_of(x, y, c)
-    count = proj_ref.shape[0]
-    per = count // NZ
-    step = PLANE_GROUP * per
-    factor = SCALE * LOG2E
-    top_ref[...] = jnp.full(top_ref.shape, NEG, F32)
-    acc_ref[...] = jnp.zeros(acc_ref.shape, F32)
-    width = KEY_GROUP * step
-    ones = jnp.ones((width, HE), BF)
-    t = lax.broadcasted_iota(jnp.int32, (step, 1), 0)
-    u = lax.broadcasted_iota(jnp.int32, (1, width), 1)
-    t_order = (t // per * NP + me) * 32 + t % per
-    u_order = u % step // per * (NP * 32) + u % per
-
-    def attend(slots):
-        order = u_order
-        for i, slot in enumerate(slots):
-            order = jnp.where(u // step == i, order + slot * 32, order)
-        allowed = order <= t_order
-        for n in range(NZ // PLANE_GROUP):
-            lo = n * step
-            keys = jnp.concatenate([kv_ref[d, lo : lo + step, :HE] for d in slots], axis=0)
-            values = jnp.concatenate([kv_ref[d, lo : lo + step, HE:] for d in slots], axis=0)
-            s = lax.dot_general(
-                proj_ref[lo:, :HE], keys, TRANS, preferred_element_type=F32
-            ) * factor
-            edge = jnp.where(allowed, s[:step], NEG)
-            s = jnp.concatenate([edge, s[step:]], axis=0) if lo + step < count else edge
-            old = top_ref[lo:, :]
-            new = jnp.maximum(old, jnp.max(s, axis=-1, keepdims=True))
-            p = jnp.exp2(s - new).astype(BF)
-            wide = jnp.concatenate([values, ones], axis=1)
-            acc_ref[lo:, :] = acc_ref[lo:, :] * jnp.exp2(old - new) + jnp.dot(
-                p, wide, preferred_element_type=F32
-            )
-            top_ref[lo:, :] = new
-
-    def slots_at(offsets, core):
-        return [slot_of((x + a) % NX, (y + b) % NY, core) for a, b in offsets]
-
-    early = [(0, 1), (0, 3), (1, 0), (3, 0), (1, 1), (1, 3), (3, 1), (3, 3)]
-    late = [(0, 0), (0, 2), (2, 0), (2, 1), (2, 3), (1, 2), (3, 2), (2, 2)]
-    next(gather)
+    along_x = [device_at((x + d) % NX, y, z, c) for d in range(NX)]
+    along_y = [device_at(x, (y + d) % NY, z, c) for d in range(NY)]
+    partner = device_at(x, y, z, 1 - c)
+    greet(along_x[1:] + along_y[1:] + [partner] + others)
+    sends = Sends(send_sem, recv_sem)
+    base_k, base_p, base_q, base_o, base_z = 0, 4, 8, 12, 16
+    own_kv = proj_ref.at[:, HE:]
+    own_q = proj_ref.at[:, :HE]
+    mine = y * NC + c
+    for d in (2, 1, 3):
+        sends.start(base_k + d, own_kv, kv_ref.at[mine], along_y[d])
+        sends.start(base_q + d, own_q, q_ref.at[d], along_x[d])
+    sends.start(base_p, own_kv, kv_ref.at[mine], partner)
+    kv_ref[mine] = proj_ref[:, HE:]
+    q_ref[0] = proj_ref[:, :HE]
     inners = w_ref.shape[0]
     loads = [
         pltpu.make_async_copy(w_src.at[pl.ds(n * inners, inners)], w_ref.at[:, n], w_sem.at[n])
@@ -697,23 +669,88 @@
     ]
     for load in loads:
         load.start()
-    for _ in range(5):
-        next(gather)
-    attend(slots_at(early, c))
-    run_all(gather)
-    attend(slots_at(late, c))
-    attend(slots_at(early, 1 - c))
-    attend(slots_at(late, 1 - c))
-    mix_ref[...] = (acc_ref[:, :HE] / acc_ref[:, HE:]).astype(BF).reshape(mix_ref.shape)
+    for d in (1, 3, 2):
+        s = (y + NY - d) % NY * NC + c
+        sends.arrived(base_k + d, kv_ref.at[s], along_y[NY - d])
+        sends.start(base_p + d, kv_ref.at[s], kv_ref.at[s], partner)
+    sends.arrived(base_p, kv_ref.at[y * NC + 1 - c], partner)
+    for d in (1, 3, 2):
+        sends.arrived(base_p + d, kv_ref.at[(y + NY - d) % NY * NC + 1 - c], partner)
+    count = proj_ref.shape[0]
+    per = count // NZ
+    step = PLANE_GROUP * per
+    factor = SCALE * LOG2E
+    side = NY * NC
+    width = side * step
+    ones = jnp.ones((width, HE), BF)
+    t = lax.broadcasted_iota(jnp.int32, (step, 1), 0)
+    u = lax.broadcasted_iota(jnp.int32, (1, width), 1)
+    t_order = t // per * (NP * 32) + t % per
+    u_order = (u % step // per * NP + u // step) * 32 + u % per
+    lane = lax.broadcasted_iota(jnp.int32, (count, HE), 1)
+
+    def attend(d):
+        owner = slot_of((x + NX - d) % NX, y, c)
+        allowed = u_order <= t_order + (owner - side * x) * 32
+        for n in range(NZ // PLANE_GROUP):
+            lo = n * step
+            keys = kv_ref[:, lo : lo + step, :HE].reshape(width, HE)
+            values = kv_ref[:, lo : lo + step, HE:].reshape(width, HE)
+            s = lax.dot_general(
+                q_ref[d, lo:, :], keys, TRANS, preferred_element_type=F32
+            ) * factor
+            edge = jnp.where(allowed, s[:step], NEG)
+            s = jnp.concatenate([edge, s[step:]], axis=0) if lo + step < count else edge
+            best = jnp.max(s, axis=-1, keepdims=True)
+            wide = jnp.concatenate([values, ones], axis=1)
+            if n == 0:
+                top_ref[...] = best
+                acc_ref[...] = jnp.dot(
+                    jnp.exp2(s - best).astype(BF), wide, preferred_element_type=F32
+                )
+            else:
+                old = top_ref[lo:, :]
+                new = jnp.maximum(old, best)
+                acc_ref[lo:, :] = acc_ref[lo:, :] * jnp.exp2(old - new) + jnp.dot(
+                    jnp.exp2(s - new).astype(BF), wide, preferred_element_type=F32
+                )
+                top_ref[lo:, :] = new
+        weight = top_ref[...] + jnp.log2(acc_ref[:, HE:])
+        return acc_ref[:, :HE] / acc_ref[:, HE:], weight
+
+    for d in (2, 1, 3):
+        sends.arrived(base_q + d, q_ref.at[d], along_x[NX - d])
+        mixed, weight = attend(d)
+        high = weight.astype(BF).astype(F32)
+        middle = (weight - high).astype(BF).astype(F32)
+        low = weight - high - middle
+        pieces = jnp.where(lane < 32, high, jnp.where(lane < 64, middle, low))
+        part_out[d, :, :HE] = mixed.astype(BF)
+        part_out[d, :, HE:] = pieces.astype(BF)
+        sends.start(base_o + d, part_out.at[d], part_in.at[d], along_x[NX - d])
+    mixed, weight = attend(0)
+    parts = [(mixed, weight)]
+    for d in (2, 1, 3):
+        sends.arrived(base_o + d, part_in.at[d], along_x[d])
+        got = part_in[d, :, HE:].astype(F32)
+        weight = sum(got[:, 32 * n : 32 * n + 1] for n in range(STATS))
+        parts.append((part_in[d, :, :HE].astype(F32), weight + jnp.zeros((count, HE), F32)))
+    best = functools.reduce(jnp.maximum, [w for _, w in parts])
+    total, mixed = 0.0, 0.0
+    for m, w in parts:
+        share = jnp.exp2(w - best)
+        total += share
+        mixed += share * m
+    mix_ref[...] = (mixed / total).astype(BF).reshape(mix_ref.shape)
     for d in (8, 7, 9, 6, 10, 5, 11, 4, 12, 3, 13, 2, 14, 1, 15):
-        sends.start(d - 1, mix_ref.at[(z + d) % NZ], heads_ref.at[z], others[d - 1])
+        sends.start(base_z + d, mix_ref.at[(z + d) % NZ], heads_ref.at[z], others[d - 1])
     heads_ref[z] = mix_ref[z]
+    for load in loads:
+        load.wait()
     for d in range(1, NZ):
         origin = (z + NZ - d) % NZ
-        sends.arrived(d - 1, heads_ref.at[origin], others[NZ - d - 1])
+        sends.arrived(base_z + d, heads_ref.at[origin], others[NZ - d - 1])
     sends.drain()
-    for load in loads:
-        load.wait()
     total = pooled_ref[...].astype(F32)
     depth = 2 * HE
     for n in range(NZ // 2):
@@ -725,20 +762,24 @@
 
 def coarse_stage(proj, pooled, w):
     rows = proj.shape[0]
-    count = NZ - 1 + plane_copies((0, 1))
+    count = 16 + NZ
+    heads = pltpu.VMEM((NZ, rows // NZ, HE), BF)
+    parts = pltpu.VMEM((NX, rows, 2 * HE), BF)
     return pl.pallas_call(
         coarse_kernel,
         out_shape=jax.ShapeDtypeStruct(pooled.shape, BF),
         in_specs=[vmem_spec(), vmem_spec(), hbm_spec()],
         out_specs=vmem_spec(),
         scratch_shapes=[
-            pltpu.VMEM((NP, rows, 2 * HE), BF),
+            pltpu.VMEM((NY * NC, rows, 2 * HE), BF),
+            pltpu.VMEM((NX, rows, HE), BF),
             pltpu.VMEM((rows, 1), F32),
             pltpu.VMEM((rows, 2 * HE), F32),
-            pltpu.VMEM((NZ, rows // NZ, HE), BF),
-            pltpu.VMEM((NZ, rows // NZ, HE), BF),
+            parts,
+            parts,
+            heads,
+            heads,
             pltpu.VMEM((NP // 2, 2, *w.shape[1:]), BF),
-            pltpu.SemaphoreType.DMA,
             pltpu.SemaphoreType.DMA((2,)),
             pltpu.SemaphoreType.DMA((count,)),
             pltpu.SemaphoreType.DMA((count,)),
@@ -763,10 +804,10 @@
     w_coarse_out,
 ):
     rows, width = fine_input.shape
-    state, pooled, normed, w_head = fine_stage(
-        fine_input, fine_query, fine_key, fine_value, norm_gain, w_fine_out, w_query, w_key, w_value
+    state, pooled, normed = fine_stage(
+        fine_input, fine_query, fine_key, fine_value, norm_gain, w_fine_out
     )
-    tokens, w_out = middle_stage(normed, w_coarse_out)
+    tokens, w_out, w_head = middle_stage(normed, w_coarse_out, w_query, w_key, w_value)
     proj = jnp.dot(
         tokens.reshape(-1, width), w_head.reshape(width, -1), preferred_element_type=F32
     ).astype(BF)

time: 159 us -> 154 us (0.969)
  Pallas kernels: 156 us -> 151 us
    pallas_call x1, Pallas kernels: 71.1 us -> 45.1 us  [fine_stage(): pl.pallas_call(fine_kernel, out_shape=[jax.ShapeDtypeStruct((rows, width)...]
    pallas_call x1, Pallas kernels: 41.4 us -> 63 us  [middle_stage(): pl.pallas_call(middle_kernel, out_shape=[jax.ShapeDtypeStruct((NZ, *norme...]
where the time goes in v4:
time: 154 us
  Pallas kernels  151 us (98%)
    pallas_call x1, Pallas kernels, middle_stage(): pl.pallas_call(middle_kernel, out_shape=[jax.ShapeDtypeStruct((NZ, *norme...  63 us
    pallas_call x1, Pallas kernels, fine_stage(): pl.pallas_call(fine_kernel, out_shape=[jax.ShapeDtypeStruct((rows, width)...  45.1 us
    pallas_call x1, Pallas kernels, coarse_stage(): pl.pallas_call(coarse_kernel, out_shape=jax.ShapeDtypeStruct(pooled.shape...  42.9 us

profile of v4, /device:TPU:1, one launch (start us, length us, event | category | flops | bytes accessed | tf_op | source)
XLA Modules:
  0.0 153.9 jit_solution(5948804616643958088)
XLA Ops:
  0.0 0.0 copy-start
  0.0 0.7 copy-done
  0.7 45.1 %fine.1 = (bf16[192,2048]{1,0:T(8,128)(2,1)S(1)}, bf16[24,2048]{1,0:T(8,128)(2,1)S(1)}, bf16[24,2048]{1,0:T(8,128)(2,1)S(1)}) custom-call(f32[1,2048]{1,0:T(1,128)S(1)} %bitcast.9, bf16[192,2048]{1,0:T(8,128)(2,1)} %x_src.1, bf16[192,1024]{1,0:T(8,128)(2,1)} %q_src.1, bf16[192,1024]{1,0:T(8,128)(2,1)} %k_src.1, bf16[192,1024]{1,0:T(8,128)(2,1)} %v_src.1, ...), custom_call_target="tpu_custom_call" | custom-call | tf_op jit(solution)/shard_map/fine/pallas_call | solution.py:437
  45.8 63.0 %middle.1 = (bf16[16,24,2048]{2,1,0:T(8,128)(2,1)S(1)}, bf16[32,64,2048]{2,1,0:T(8,128)(2,1)S(1)}, bf16[32,64,384]{2,1,0:T(8,128)(2,1)S(1)}) custom-call(bf16[24,2048]{1,0:T(8,128)(2,1)S(1)} %get-tuple-element.12.normed_ref, bf16[128,2048]{1,0:T(8,128)(2,1)} %w_src.3, bf16[2048,128]{1,0:T(8,128)(2,1)} %wq_ref.1, bf16[2048,128]{1,0:T(8,128)(2,1)} %wk_ref.1, ...), custom_call_target="tpu_custom_call" | custom-call | tf_op jit(solution)/shard_map/middle/pallas_call | solution.py:615
  108.9 1.0 convolution_convert_fusion.proj_ref
  109.9 42.9 %coarse.1 = bf16[24,2048]{1,0:T(8,128)(2,1)S(1)} custom-call(bf16[384,384]{1,0:T(8,128)(2,1)S(1)} %convolution_convert_fusion.proj_ref, bf16[24,2048]{1,0:T(8,128)(2,1)S(1)} %get-tuple-element.15.pooled_ref, bf16[32,64,2048]{2,1,0:T(8,128)(2,1)S(1)} %get-tuple-element.16.w_src), custom_call_target="tpu_custom_call" | custom-call | tf_op jit(solution)/shard_map/coarse/pallas_call | solution.py:768
  152.8 1.1 fusion
  (1 shorter events, 0.0 us)
Async XLA Ops:
  0.0 0.7 copy-start

commit v5 on v4

--- a/solution.py
+++ b/solution.py
@@ -584,75 +584,46 @@
     yield
 
 
-def middle_kernel(
-    normed_ref, w_src, wq_ref, wk_ref, wv_ref, tokens_ref, w_ref, head_ref,
-    piece_ref, local_sem, scatter_send, scatter_recv, send_sem, recv_sem,
+PLANE_GROUP = 4
+STATS = 3
+
+
+def coarse_kernel(
+    normed_ref, pooled_ref, w_src, wq_ref, wk_ref, wv_ref, out_ref,
+    tokens_ref, w_ref, head_ref, piece_ref, proj_ref,
+    kv_ref, q_ref, top_ref, acc_ref, part_out, part_in, mix_ref, heads_ref,
+    local_sem, scatter_send, scatter_recv, send_sem, recv_sem,
 ):
     x, y, z, c = place()
     outer = lax.axis_index("outer")
     inner = lax.axis_index("inner")
     plane = [(a, b) for a in range(NX) for b in range(NY)][1:]
+    others = [device_at(x, y, (z + d) % NZ, c) for d in range(1, NZ)]
+    along_x = [device_at((x + d) % NX, y, z, c) for d in range(NX)]
+    along_y = [device_at(x, (y + d) % NY, z, c) for d in range(NY)]
+    partner = device_at(x, y, z, 1 - c)
     greet(
         [device_at((x + a) % NX, (y + b) % NY, z, c) for a, b in plane]
-        + [device_at(x, y, z, 1 - c)]
-        + [device_at(x, y, (z + d + NZ) % NZ, c) for d in (1, -1)]
+        + [partner]
+        + others
         + [(outer, (inner + d) % 16) for d in range(1, 16)]
     )
-    sends = Sends(send_sem, recv_sem)
+    base_k, base_p, base_q, base_o, base_z = 0, 4, 8, 12, 16
+    sends = Sends(send_sem, recv_sem, base_z + NZ)
     along = z_gather(sends, normed_ref, tokens_ref, local_sem.at[0])
     out = plane_gather(sends, half_rows(w_src), w_ref, local_sem.at[1])
     pieces = scatter((wq_ref, wk_ref, wv_ref), piece_ref, local_sem.at[pl.ds(2, 3)], scatter_send, scatter_recv)
     head = to_all_of_plane(sends, piece_ref, head_ref, local_sem.at[5])
     order = (along, pieces, out, along, along, pieces, head, out, along, out, along, out, along, out)
-    for steps in order + (along, head, along, out, along, head, out):
+    for steps in order + (along, head, along, along, head):
         next(steps)
-    sends.drain()
-
-
-def middle_stage(normed, w, *head_weights):
-    count = z_copies(normed.shape[0]) + plane_copies((0, 1)) + PIECE_COPIES
-    piece = (normed.shape[1] // NP, len(head_weights) * HE)
-    return pl.pallas_call(
-        middle_kernel,
-        out_shape=[
-            jax.ShapeDtypeStruct((NZ, *normed.shape), BF),
-            jax.ShapeDtypeStruct((NP, w.shape[0] // 2, w.shape[1]), BF),
-            jax.ShapeDtypeStruct((NP, *piece), BF),
-        ],
-        in_specs=[any_spec()] + [hbm_spec()] * 4,
-        out_specs=[any_spec(), hbm_spec(), any_spec()],
-        scratch_shapes=[
-            pltpu.VMEM(piece, BF),
-            pltpu.SemaphoreType.DMA((6,)),
-            pltpu.SemaphoreType.DMA((3, 15)),
-            pltpu.SemaphoreType.DMA((3,)),
-            pltpu.SemaphoreType.DMA((count,)),
-            pltpu.SemaphoreType.DMA((count,)),
-        ],
-        compiler_params=pltpu.CompilerParams(
-            collective_id=3, has_side_effects=True, vmem_limit_bytes=16 << 20
-        ),
-        name="middle",
-    )(normed, *[in_hbm(a) for a in (w, *head_weights)])
-
-
-PLANE_GROUP = 4
-STATS = 3
-
-
-def coarse_kernel(
-    proj_ref, pooled_ref, w_src, out_ref,
-    kv_ref, q_ref, top_ref, acc_ref, part_out, part_in, mix_ref, heads_ref, w_ref,
-    w_sem, send_sem, recv_sem,
-):
-    x, y, z, c = place()
-    others = [device_at(x, y, (z + d) % NZ, c) for d in range(1, NZ)]
-    along_x = [device_at((x + d) % NX, y, z, c) for d in range(NX)]
-    along_y = [device_at(x, (y + d) % NY, z, c) for d in range(NY)]
-    partner = device_at(x, y, z, 1 - c)
-    greet(along_x[1:] + along_y[1:] + [partner] + others)
-    sends = Sends(send_sem, recv_sem)
-    base_k, base_p, base_q, base_o, base_z = 0, 4, 8, 12, 16
+    count = proj_ref.shape[0]
+    deep = tokens_ref.shape[2]
+    proj_ref[...] = jnp.dot(
+        tokens_ref[...].reshape(count, deep),
+        head_ref[...].reshape(deep, proj_ref.shape[1]),
+        preferred_element_type=F32,
+    ).astype(BF)
     own_kv = proj_ref.at[:, HE:]
     own_q = proj_ref.at[:, :HE]
     mine = y * NC + c
@@ -662,13 +633,7 @@
     sends.start(base_p, own_kv, kv_ref.at[mine], partner)
     kv_ref[mine] = proj_ref[:, HE:]
     q_ref[0] = proj_ref[:, :HE]
-    inners = w_ref.shape[0]
-    loads = [
-        pltpu.make_async_copy(w_src.at[pl.ds(n * inners, inners)], w_ref.at[:, n], w_sem.at[n])
-        for n in range(w_ref.shape[1])
-    ]
-    for load in loads:
-        load.start()
+    next(out)
     for d in (1, 3, 2):
         s = (y + NY - d) % NY * NC + c
         sends.arrived(base_k + d, kv_ref.at[s], along_y[NY - d])
@@ -676,7 +641,6 @@
     sends.arrived(base_p, kv_ref.at[y * NC + 1 - c], partner)
     for d in (1, 3, 2):
         sends.arrived(base_p + d, kv_ref.at[(y + NY - d) % NY * NC + 1 - c], partner)
-    count = proj_ref.shape[0]
     per = count // NZ
     step = PLANE_GROUP * per
     factor = SCALE * LOG2E
@@ -745,32 +709,38 @@
     for d in (8, 7, 9, 6, 10, 5, 11, 4, 12, 3, 13, 2, 14, 1, 15):
         sends.start(base_z + d, mix_ref.at[(z + d) % NZ], heads_ref.at[z], others[d - 1])
     heads_ref[z] = mix_ref[z]
-    for load in loads:
-        load.wait()
+    next(out)
     for d in range(1, NZ):
         origin = (z + NZ - d) % NZ
         sends.arrived(base_z + d, heads_ref.at[origin], others[NZ - d - 1])
     sends.drain()
     total = pooled_ref[...].astype(F32)
-    depth = 2 * HE
     for n in range(NZ // 2):
         two = jnp.concatenate([heads_ref[2 * n], heads_ref[2 * n + 1]], axis=1)
-        w = w_ref[2 * n : 2 * n + 2].reshape(depth, total.shape[1])
+        rows = [w_ref[h + half] for h in (2 * n, 2 * n + 1) for half in (0, NP // 2)]
+        w = jnp.concatenate(rows, axis=0)
         total += jnp.dot(two, w, preferred_element_type=F32)
     out_ref[...] = total.astype(BF)
 
 
-def coarse_stage(proj, pooled, w):
-    rows = proj.shape[0]
-    count = 16 + NZ
+def coarse_stage(normed, pooled, w, *head_weights):
+    width = normed.shape[1]
+    rows = NZ * normed.shape[0]
+    count = 16 + NZ + z_copies(normed.shape[0]) + plane_copies((0, 1)) + PIECE_COPIES
+    piece = (width // NP, len(head_weights) * HE)
     heads = pltpu.VMEM((NZ, rows // NZ, HE), BF)
     parts = pltpu.VMEM((NX, rows, 2 * HE), BF)
     return pl.pallas_call(
         coarse_kernel,
         out_shape=jax.ShapeDtypeStruct(pooled.shape, BF),
-        in_specs=[vmem_spec(), vmem_spec(), hbm_spec()],
+        in_specs=[vmem_spec(), vmem_spec()] + [hbm_spec()] * 4,
         out_specs=vmem_spec(),
         scratch_shapes=[
+            pltpu.VMEM((NZ, *normed.shape), BF),
+            pltpu.VMEM((NP, w.shape[0] // 2, width), BF),
+            pltpu.VMEM((NP, *piece), BF),
+            pltpu.VMEM(piece, BF),
+            pltpu.VMEM((rows, piece[1]), BF),
             pltpu.VMEM((NY * NC, rows, 2 * HE), BF),
             pltpu.VMEM((NX, rows, HE), BF),
             pltpu.VMEM((rows, 1), F32),
@@ -779,16 +749,17 @@
             parts,
             heads,
             heads,
-            pltpu.VMEM((NP // 2, 2, *w.shape[1:]), BF),
-            pltpu.SemaphoreType.DMA((2,)),
+            pltpu.SemaphoreType.DMA((6,)),
+            pltpu.SemaphoreType.DMA((3, 15)),
+            pltpu.SemaphoreType.DMA((3,)),
             pltpu.SemaphoreType.DMA((count,)),
             pltpu.SemaphoreType.DMA((count,)),
         ],
         compiler_params=pltpu.CompilerParams(
-            collective_id=4, has_side_effects=True, vmem_limit_bytes=36 << 20
+            collective_id=4, has_side_effects=True, vmem_limit_bytes=40 << 20
         ),
         name="coarse",
-    )(proj, pooled, w)
+    )(normed, pooled, *[in_hbm(a) for a in (w, *head_weights)])
 
 
 def on_device(
@@ -807,11 +778,7 @@
     state, pooled, normed = fine_stage(
         fine_input, fine_query, fine_key, fine_value, norm_gain, w_fine_out
     )
-    tokens, w_out, w_head = middle_stage(normed, w_coarse_out, w_query, w_key, w_value)
-    proj = jnp.dot(
-        tokens.reshape(-1, width), w_head.reshape(width, -1), preferred_element_type=F32
-    ).astype(BF)
-    coarse_out = coarse_stage(proj, pooled, w_out)
+    coarse_out = coarse_stage(normed, pooled, w_coarse_out, w_query, w_key, w_value)
     groups = state.reshape(rows // POOL, POOL, width).astype(F32)
     lifted = groups + coarse_out.astype(F32)[:, None, :]
     return lifted.reshape(rows, width).astype(BF)

time: 154 us -> 143 us (0.929)
  Pallas kernels: 151 us -> 141 us
    pallas_call x1 -> x0, Pallas kernels: 63 us -> none  [middle_stage(): pl.pallas_call(middle_kernel, out_shape=[jax.ShapeDtypeStruct((NZ, *norme...]
    pallas_call x1, Pallas kernels: 42.9 us -> 95.5 us  [coarse_stage(): pl.pallas_call(coarse_kernel, out_shape=jax.ShapeDtypeStruct(pooled.shape...]
where the time goes in v5:
time: 143 us; the launch traced here: 142 us
  Pallas kernels  141 us (99%)
    pallas_call x1, Pallas kernels, coarse_stage(): pl.pallas_call(coarse_kernel, out_shape=jax.ShapeDtypeStruct(pooled.shape...  95.5 us
    pallas_call x1, Pallas kernels, fine_stage(): pl.pallas_call(fine_kernel, out_shape=[jax.ShapeDtypeStruct((rows, width)...  45.1 us

profile of v5, /device:TPU:1, one launch (start us, length us, event | category | flops | bytes accessed | tf_op | source)
XLA Modules:
  0.0 142.5 jit_solution(3465592729014414618)
XLA Ops:
  0.0 0.0 copy-start
  0.0 0.7 copy-done
  0.7 45.1 %fine.1 = (bf16[192,2048]{1,0:T(8,128)(2,1)S(1)}, bf16[24,2048]{1,0:T(8,128)(2,1)S(1)}, bf16[24,2048]{1,0:T(8,128)(2,1)S(1)}) custom-call(f32[1,2048]{1,0:T(1,128)S(1)} %bitcast.5, bf16[192,2048]{1,0:T(8,128)(2,1)} %x_src.1, bf16[192,1024]{1,0:T(8,128)(2,1)} %q_src.1, bf16[192,1024]{1,0:T(8,128)(2,1)} %k_src.1, bf16[192,1024]{1,0:T(8,128)(2,1)} %v_src.1, ...), custom_call_target="tpu_custom_call" | custom-call | tf_op jit(solution)/shard_map/fine/pallas_call | solution.py:437
  45.8 95.5 %coarse.1 = bf16[24,2048]{1,0:T(8,128)(2,1)S(1)} custom-call(bf16[24,2048]{1,0:T(8,128)(2,1)S(1)} %get-tuple-element.9.normed_ref, bf16[24,2048]{1,0:T(8,128)(2,1)S(1)} %get-tuple-element.10.pooled_ref, bf16[128,2048]{1,0:T(8,128)(2,1)} %w_src.3, bf16[2048,128]{1,0:T(8,128)(2,1)} %wq_ref.1, bf16[2048,128]{1,0:T(8,128)(2,1)} %wk_ref.1, bf16[2048,128]{1,0:T(8,128)(2,1)} %wv_ref.1), custom_call_target="tpu_custom_call" | custom-call | tf_op jit(solution)/shard_map/coarse/pallas_call | solution.py:733
  141.4 1.1 fusion
  (1 shorter events, 0.0 us)
Async XLA Ops:
  0.0 0.7 copy-start

commit v6 on v5

--- a/solution.py
+++ b/solution.py
@@ -330,21 +330,17 @@
     return jnp.where(c == 1, to_o, by_o), jnp.where(c == 1, to_i, by_i)
 
 
-def fine_kernel(
+def fine_part(
+    sends, background,
     gain_ref, x_src, q_src, k_src, v_src, w_src,
     state_ref, pooled_ref, normed_ref,
     x_ref, q_ref, k_ref, v_ref, mix_ref, edge_out, edge_in, kp_ref, vp_ref, relay_ref, w_ref,
     load_sem, local_sem, send_sem, recv_sem,
 ):
+    pieces, head, out = background
     rows = q_ref.shape[0]
     heads = q_ref.shape[1] // HE
     position = lax.axis_index("outer") * 16 + lax.axis_index("inner")
-    greet(
-        plane_neighbours()
-        + [device_of(position + d) for d in (2, -2, 1, -1)]
-        + [relay_target()]
-    )
-    sends = Sends(send_sem, recv_sem, HALO_COPIES)
     weights = plane_gather(sends, half_rows(w_src), w_ref, local_sem, W_FIRSTS)
     before_rows = halo_copies(sends, k_src, v_src, kp_ref, vp_ref, relay_ref)
     loads = [
@@ -358,13 +354,21 @@
     next(before_rows)
     for load in loads:
         load.start()
-    for steps in (weights, before_rows, before_rows, weights, before_rows, before_rows, weights):
+    for steps in (weights, before_rows, before_rows, pieces, weights, before_rows, before_rows, weights):
         next(steps)
     for steps in (before_rows,) * 4 + (weights,) + (before_rows,) * 2:
         next(steps)
     for load in loads:
         load.wait()
-    between = {0: (weights,), 1: (before_rows,), 2: (before_rows,), 3: (before_rows,) * 2, 5: (weights,)}
+    between = {
+        0: (weights,),
+        1: (before_rows,),
+        2: (before_rows,),
+        3: (before_rows, before_rows, pieces, head),
+        4: (out,),
+        5: (weights,),
+        7: (out,),
+    }
     t_prev = lax.broadcasted_iota(jnp.int32, (rows, WIN), 0)
     u_prev = lax.broadcasted_iota(jnp.int32, (rows, WIN), 1)
     ok_prev = (u_prev > t_prev) & (position * rows - WIN + u_prev >= 0)
@@ -413,9 +417,12 @@
         device_id_type=MESH,
     )
     send.start()
+    next(head)
+    next(out)
     groups = state_ref[...].astype(F32).reshape(rows // POOL, POOL, width)
     first = groups[:, 0, :]
     rest = jnp.sum(groups[:, 1:, :], axis=1)
+    next(head)
     send.wait()
     edge = jnp.sum(edge_in[...].astype(F32)[1:, :], axis=0, keepdims=True)
     edge = jnp.where(position == 0, 0.0, edge)
@@ -425,39 +432,11 @@
     wide = pooled.astype(F32)
     moment = jnp.mean(wide * wide, axis=-1, keepdims=True)
     normed_ref[...] = (wide * lax.rsqrt(moment + 1e-06) * gain_ref[...]).astype(BF)
-    sends.drain()
-
-
-EDGE_COPY = HALO_COPIES + plane_copies(W_FIRSTS)
-
-
-def fine_stage(x, q, k, v, gain, w):
-    rows, width = x.shape
-    coarse = jax.ShapeDtypeStruct((rows // POOL, width), BF)
-    return pl.pallas_call(
-        fine_kernel,
-        out_shape=[jax.ShapeDtypeStruct((rows, width), BF), coarse, coarse],
-        in_specs=[vmem_spec()] + [hbm_spec()] * 5,
-        out_specs=[vmem_spec()] * 3,
-        scratch_shapes=[
-            *[pltpu.VMEM(a.shape, BF) for a in (x, q, k, v)],
-            pltpu.VMEM(q.shape, BF),
-            pltpu.VMEM((POOL, width), BF),
-            pltpu.VMEM((POOL, width), BF),
-            pltpu.VMEM((WIN, k.shape[1]), BF),
-            pltpu.VMEM((WIN, k.shape[1]), BF),
-            pltpu.VMEM((HALO_PARTS, WIN - 2 * rows, k.shape[1] // 2), BF),
-            pltpu.VMEM((NP, w.shape[0] // 2, w.shape[1]), BF),
-            pltpu.SemaphoreType.DMA((4,)),
-            pltpu.SemaphoreType.DMA,
-            pltpu.SemaphoreType.DMA((EDGE_COPY + 1,)),
-            pltpu.SemaphoreType.DMA((EDGE_COPY + 1,)),
-        ],
-        compiler_params=pltpu.CompilerParams(
-            collective_id=2, has_side_effects=True, vmem_limit_bytes=32 << 20
-        ),
-        name="fine",
-    )(gain.reshape(1, width), *[in_hbm(a) for a in (x, q, k, v, w)])
+
+
+EDGE_COPY = HALO_COPIES
+EXCHANGE_COPY = EDGE_COPY + 1
+FIXED_COPIES = EXCHANGE_COPY + 32
 
 
 ZCHUNK = 8
@@ -588,34 +567,20 @@
 STATS = 3
 
 
-def coarse_kernel(
-    normed_ref, pooled_ref, w_src, wq_ref, wk_ref, wv_ref, out_ref,
-    tokens_ref, w_ref, head_ref, piece_ref, proj_ref,
-    kv_ref, q_ref, top_ref, acc_ref, part_out, part_in, mix_ref, heads_ref,
-    local_sem, scatter_send, scatter_recv, send_sem, recv_sem,
+def coarse_part(
+    sends, out,
+    normed_ref, pooled_ref, out_ref,
+    tokens_ref, w_ref, head_ref, proj_ref,
+    kv_ref, q_ref, top_ref, acc_ref, part_out, part_in, mix_ref, heads_ref, local_sem,
 ):
     x, y, z, c = place()
-    outer = lax.axis_index("outer")
-    inner = lax.axis_index("inner")
-    plane = [(a, b) for a in range(NX) for b in range(NY)][1:]
     others = [device_at(x, y, (z + d) % NZ, c) for d in range(1, NZ)]
     along_x = [device_at((x + d) % NX, y, z, c) for d in range(NX)]
     along_y = [device_at(x, (y + d) % NY, z, c) for d in range(NY)]
     partner = device_at(x, y, z, 1 - c)
-    greet(
-        [device_at((x + a) % NX, (y + b) % NY, z, c) for a, b in plane]
-        + [partner]
-        + others
-        + [(outer, (inner + d) % 16) for d in range(1, 16)]
-    )
-    base_k, base_p, base_q, base_o, base_z = 0, 4, 8, 12, 16
-    sends = Sends(send_sem, recv_sem, base_z + NZ)
-    along = z_gather(sends, normed_ref, tokens_ref, local_sem.at[0])
-    out = plane_gather(sends, half_rows(w_src), w_ref, local_sem.at[1])
-    pieces = scatter((wq_ref, wk_ref, wv_ref), piece_ref, local_sem.at[pl.ds(2, 3)], scatter_send, scatter_recv)
-    head = to_all_of_plane(sends, piece_ref, head_ref, local_sem.at[5])
-    order = (along, pieces, out, along, along, pieces, head, out, along, out, along, out, along, out)
-    for steps in order + (along, head, along, along, head):
+    base_k, base_p, base_q, base_o, base_z = (EXCHANGE_COPY + n for n in (0, 4, 8, 12, 16))
+    along = z_gather(sends, normed_ref, tokens_ref, local_sem)
+    for steps in (along,) * 3 + (out, along, along, out, along, along, along, along):
         next(steps)
     count = proj_ref.shape[0]
     deep = tokens_ref.shape[2]
@@ -723,43 +688,98 @@
     out_ref[...] = total.astype(BF)
 
 
-def coarse_stage(normed, pooled, w, *head_weights):
-    width = normed.shape[1]
-    rows = NZ * normed.shape[0]
-    count = 16 + NZ + z_copies(normed.shape[0]) + plane_copies((0, 1)) + PIECE_COPIES
+def layer_kernel(
+    gain_ref, x_src, q_src, k_src, v_src, w_fine, w_out, wq_ref, wk_ref, wv_ref,
+    state_ref, out_ref,
+    x_ref, q_ref, k_ref, v_ref, fine_mix, edge_out, edge_in, kp_ref, vp_ref, relay_ref, w_fine_all,
+    pooled_ref, normed_ref, tokens_ref, w_out_all, head_ref, piece_ref, proj_ref,
+    kv_ref, cq_ref, top_ref, acc_ref, part_out, part_in, mix_ref, heads_ref,
+    load_sem, local_sem, scatter_send, scatter_recv, send_sem, recv_sem,
+):
+    x, y, z, c = place()
+    outer = lax.axis_index("outer")
+    inner = lax.axis_index("inner")
+    position = outer * 16 + inner
+    plane = [(a, b) for a in range(NX) for b in range(NY)][1:]
+    greet(
+        [device_at((x + a) % NX, (y + b) % NY, z, c) for a, b in plane]
+        + [device_at(x, y, z, 1 - c)]
+        + [device_at(x, y, (z + d) % NZ, c) for d in range(1, NZ)]
+        + [(outer, (inner + d) % 16) for d in range(1, 16)]
+        + [device_of(position + d) for d in (2, -2, 1, -1)]
+        + [relay_target()]
+    )
+    sends = Sends(send_sem, recv_sem, FIXED_COPIES)
+    pieces = scatter((wq_ref, wk_ref, wv_ref), piece_ref, local_sem.at[pl.ds(2, 3)], scatter_send, scatter_recv)
+    head = to_all_of_plane(sends, piece_ref, head_ref, local_sem.at[5])
+    out = plane_gather(sends, half_rows(w_out), w_out_all, local_sem.at[1])
+    fine_part(
+        sends, (pieces, head, out),
+        gain_ref, x_src, q_src, k_src, v_src, w_fine,
+        state_ref, pooled_ref, normed_ref,
+        x_ref, q_ref, k_ref, v_ref, fine_mix, edge_out, edge_in, kp_ref, vp_ref, relay_ref, w_fine_all,
+        load_sem, local_sem.at[6], send_sem, recv_sem,
+    )
+    coarse_part(
+        sends, out,
+        normed_ref, pooled_ref, out_ref,
+        tokens_ref, w_out_all, head_ref, proj_ref,
+        kv_ref, cq_ref, top_ref, acc_ref, part_out, part_in, mix_ref, heads_ref, local_sem.at[0],
+    )
+
+
+def layer_stage(x, q, k, v, gain, w_fine, w_out, *head_weights):
+    rows, width = x.shape
+    per = rows // POOL
+    tokens = NZ * per
+    block = (per, width)
     piece = (width // NP, len(head_weights) * HE)
-    heads = pltpu.VMEM((NZ, rows // NZ, HE), BF)
-    parts = pltpu.VMEM((NX, rows, 2 * HE), BF)
+    heads = pltpu.VMEM((NZ, per, HE), BF)
+    parts = pltpu.VMEM((NX, tokens, 2 * HE), BF)
+    edge = pltpu.VMEM((POOL, width), BF)
+    before = pltpu.VMEM((WIN, k.shape[1]), BF)
+    count = FIXED_COPIES + plane_copies(W_FIRSTS) + plane_copies((0, 1)) + PIECE_COPIES + z_copies(per)
     return pl.pallas_call(
-        coarse_kernel,
-        out_shape=jax.ShapeDtypeStruct(pooled.shape, BF),
-        in_specs=[vmem_spec(), vmem_spec()] + [hbm_spec()] * 4,
-        out_specs=vmem_spec(),
+        layer_kernel,
+        out_shape=[jax.ShapeDtypeStruct((rows, width), BF), jax.ShapeDtypeStruct(block, BF)],
+        in_specs=[vmem_spec()] + [hbm_spec()] * 9,
+        out_specs=[vmem_spec()] * 2,
         scratch_shapes=[
-            pltpu.VMEM((NZ, *normed.shape), BF),
-            pltpu.VMEM((NP, w.shape[0] // 2, width), BF),
+            *[pltpu.VMEM(a.shape, BF) for a in (x, q, k, v)],
+            pltpu.VMEM(q.shape, BF),
+            edge,
+            edge,
+            before,
+            before,
+            pltpu.VMEM((HALO_PARTS, WIN - 2 * rows, k.shape[1] // 2), BF),
+            pltpu.VMEM((NP, w_fine.shape[0] // 2, w_fine.shape[1]), BF),
+            pltpu.VMEM(block, BF),
+            pltpu.VMEM(block, BF),
+            pltpu.VMEM((NZ, *block), BF),
+            pltpu.VMEM((NP, w_out.shape[0] // 2, width), BF),
             pltpu.VMEM((NP, *piece), BF),
             pltpu.VMEM(piece, BF),
-            pltpu.VMEM((rows, piece[1]), BF),
-            pltpu.VMEM((NY * NC, rows, 2 * HE), BF),
-            pltpu.VMEM((NX, rows, HE), BF),
-            pltpu.VMEM((rows, 1), F32),
-            pltpu.VMEM((rows, 2 * HE), F32),
+            pltpu.VMEM((tokens, piece[1]), BF),
+            pltpu.VMEM((NY * NC, tokens, 2 * HE), BF),
+            pltpu.VMEM((NX, tokens, HE), BF),
+            pltpu.VMEM((tokens, 1), F32),
+            pltpu.VMEM((tokens, 2 * HE), F32),
             parts,
             parts,
             heads,
             heads,
-            pltpu.SemaphoreType.DMA((6,)),
+            pltpu.SemaphoreType.DMA((4,)),
+            pltpu.SemaphoreType.DMA((7,)),
             pltpu.SemaphoreType.DMA((3, 15)),
             pltpu.SemaphoreType.DMA((3,)),
             pltpu.SemaphoreType.DMA((count,)),
             pltpu.SemaphoreType.DMA((count,)),
         ],
         compiler_params=pltpu.CompilerParams(
-            collective_id=4, has_side_effects=True, vmem_limit_bytes=40 << 20
+            collective_id=4, has_side_effects=True, vmem_limit_bytes=52 << 20
         ),
-        name="coarse",
-    )(normed, pooled, *[in_hbm(a) for a in (w, *head_weights)])
+        name="layer",
+    )(gain.reshape(1, width), *[in_hbm(a) for a in (x, q, k, v, w_fine, w_out, *head_weights)])
 
 
 def on_device(
@@ -775,10 +795,10 @@
     w_coarse_out,
 ):
     rows, width = fine_input.shape
-    state, pooled, normed = fine_stage(
-        fine_input, fine_query, fine_key, fine_value, norm_gain, w_fine_out
+    state, coarse_out = layer_stage(
+        fine_input, fine_query, fine_key, fine_value, norm_gain,
+        w_fine_out, w_coarse_out, w_query, w_key, w_value,
     )
-    coarse_out = coarse_stage(normed, pooled, w_coarse_out, w_query, w_key, w_value)
     groups = state.reshape(rows // POOL, POOL, width).astype(F32)
     lifted = groups + coarse_out.astype(F32)[:, None, :]
     return lifted.reshape(rows, width).astype(BF)

time: 143 us -> 148 us (1.035)
  the two profiles are of different devices: /device:TPU:1 before, /device:TPU:8 now
where the time goes in v6:
time: 148 us
  Pallas kernels  146 us (99%)
    pallas_call x1, Pallas kernels, layer_stage(): pl.pallas_call(layer_kernel, out_shape=[jax.ShapeDtypeStruct((rows, width...  146 us

profile of v6, /device:TPU:8, one launch (start us, length us, event | category | flops | bytes accessed | tf_op | source)
XLA Modules:
  0.0 147.9 jit_solution(9199837935658576893)
XLA Ops:
  0.0 0.0 copy-start
  0.0 0.7 copy-done
  0.7 146.1 %layer.1 = (bf16[192,2048]{1,0:T(8,128)(2,1)S(1)}, bf16[24,2048]{1,0:T(8,128)(2,1)S(1)}) custom-call(f32[1,2048]{1,0:T(1,128)S(1)} %bitcast.5, bf16[192,2048]{1,0:T(8,128)(2,1)} %x_src.1, bf16[192,1024]{1,0:T(8,128)(2,1)} %q_src.1, bf16[192,1024]{1,0:T(8,128)(2,1)} %k_src.1, bf16[192,1024]{1,0:T(8,128)(2,1)} %v_src.1, bf16[1024,128]{1,0:T(8,128)(2,1)} %w_fine.1, ...), custom_call_target="tpu_custom_call" | custom-call | tf_op jit(solution)/shard_map/layer/pallas_call | solution.py:742
  146.8 1.1 fusion
  (1 shorter events, 0.0 us)
Async XLA Ops:
  0.0 0.7 copy-start

commit v7 on v5

--- a/solution.py
+++ b/solution.py
@@ -365,28 +365,38 @@
     for load in loads:
         load.wait()
     between = {0: (weights,), 1: (before_rows,), 2: (before_rows,), 3: (before_rows,) * 2, 5: (weights,)}
-    t_prev = lax.broadcasted_iota(jnp.int32, (rows, WIN), 0)
-    u_prev = lax.broadcasted_iota(jnp.int32, (rows, WIN), 1)
-    ok_prev = (u_prev > t_prev) & (position * rows - WIN + u_prev >= 0)
+    near = WIN // 2
+    t_far = lax.broadcasted_iota(jnp.int32, (rows, near), 0)
+    u_far = lax.broadcasted_iota(jnp.int32, (rows, near), 1)
+    first_row = WIN - position * rows
+    ok_far = (u_far > t_far) & (u_far >= first_row)
+    ok_near = lax.broadcasted_iota(jnp.int32, (1, near), 1) + near >= first_row
     t_own = lax.broadcasted_iota(jnp.int32, (rows, rows), 0)
     u_own = lax.broadcasted_iota(jnp.int32, (rows, rows), 1)
     ok_own = u_own <= t_own
+    factor = SCALE * LOG2E
     for h in range(heads):
         cols = slice(h * HE, (h + 1) * HE)
         q = q_ref[:, cols]
-        s_prev = lax.dot_general(q, kp_ref[:, cols], TRANS, preferred_element_type=F32) * SCALE
-        s_own = lax.dot_general(q, k_ref[:, cols], TRANS, preferred_element_type=F32) * SCALE
-        s_prev = jnp.where(ok_prev, s_prev, NEG)
-        s_own = jnp.where(ok_own, s_own, NEG)
-        top = jnp.maximum(
-            jnp.max(s_prev, axis=-1, keepdims=True), jnp.max(s_own, axis=-1, keepdims=True)
+        blocks = (
+            (kp_ref[:near, cols], vp_ref[:near, cols], ok_far),
+            (kp_ref[near:, cols], vp_ref[near:, cols], ok_near),
+            (k_ref[:, cols], v_ref[:, cols], ok_own),
         )
-        p_prev = jnp.exp(s_prev - top)
-        p_own = jnp.exp(s_own - top)
-        total = jnp.sum(p_prev, axis=-1, keepdims=True) + jnp.sum(p_own, axis=-1, keepdims=True)
-        mixed = jnp.dot(p_prev.astype(BF), vp_ref[:, cols], preferred_element_type=F32)
-        mixed += jnp.dot(p_own.astype(BF), v_ref[:, cols], preferred_element_type=F32)
-        mix_ref[:, cols] = (mixed / total).astype(BF)
+        scores = [
+            jnp.where(
+                ok, lax.dot_general(q, keys, TRANS, preferred_element_type=F32) * factor, NEG
+            )
+            for keys, _, ok in blocks
+        ]
+        top = functools.reduce(
+            jnp.maximum, [jnp.max(s, axis=-1, keepdims=True) for s in scores]
+        )
+        mixed = 0.0
+        for s, (_, values, _) in zip(scores, blocks):
+            wide = jnp.concatenate([values, jnp.ones((values.shape[0], HE), BF)], axis=1)
+            mixed += jnp.dot(jnp.exp2(s - top).astype(BF), wide, preferred_element_type=F32)
+        mix_ref[:, cols] = (mixed[:, :HE] / mixed[:, HE:]).astype(BF)
         for steps in between.get(h, ()):
             next(steps)
     width = x_ref.shape[1]

time: 143 us -> 143 us (level)
  no operation moved by 1% of the time
where the time goes in v7:
time: 143 us
  Pallas kernels  141 us (99%)
    pallas_call x1, Pallas kernels, coarse_stage(): pl.pallas_call(coarse_kernel, out_shape=jax.ShapeDtypeStruct(pooled.shape...  96 us
    pallas_call x1, Pallas kernels, fine_stage(): pl.pallas_call(fine_kernel, out_shape=[jax.ShapeDtypeStruct((rows, width)...  44.8 us

profile of v7, /device:TPU:1, one launch (start us, length us, event | category | flops | bytes accessed | tf_op | source)
XLA Modules:
  0.0 142.7 jit_solution(16962916044765546992)
XLA Ops:
  0.0 0.0 copy-start
  0.0 0.7 copy-done
  0.7 44.8 %fine.1 = (bf16[192,2048]{1,0:T(8,128)(2,1)S(1)}, bf16[24,2048]{1,0:T(8,128)(2,1)S(1)}, bf16[24,2048]{1,0:T(8,128)(2,1)S(1)}) custom-call(f32[1,2048]{1,0:T(1,128)S(1)} %bitcast.5, bf16[192,2048]{1,0:T(8,128)(2,1)} %x_src.1, bf16[192,1024]{1,0:T(8,128)(2,1)} %q_src.1, bf16[192,1024]{1,0:T(8,128)(2,1)} %k_src.1, bf16[192,1024]{1,0:T(8,128)(2,1)} %v_src.1, ...), custom_call_target="tpu_custom_call" | custom-call | tf_op jit(solution)/shard_map/fine/pallas_call | solution.py:447
  45.5 96.0 %coarse.1 = bf16[24,2048]{1,0:T(8,128)(2,1)S(1)} custom-call(bf16[24,2048]{1,0:T(8,128)(2,1)S(1)} %get-tuple-element.9.normed_ref, bf16[24,2048]{1,0:T(8,128)(2,1)S(1)} %get-tuple-element.10.pooled_ref, bf16[128,2048]{1,0:T(8,128)(2,1)} %w_src.3, bf16[2048,128]{1,0:T(8,128)(2,1)} %wq_ref.1, bf16[2048,128]{1,0:T(8,128)(2,1)} %wk_ref.1, bf16[2048,128]{1,0:T(8,128)(2,1)} %wv_ref.1), custom_call_target="tpu_custom_call" | custom-call | tf_op jit(solution)/shard_map/coarse/pallas_call | solution.py:743
  141.6 1.1 fusion
  (1 shorter events, 0.0 us)
Async XLA Ops:
  0.0 0.7 copy-start
